TPU v7x, 32 devices: a whole 2x2x4 slice. The times are simulated.
32 devices in a mesh: dp: 8 (over y, x, core), tensor: 4 (over z).
Axes of the slice: x: 2, y: 2, z: 4, core: 2. Of those that a mesh axis runs over, the one named last changes fastest.
Arguments:
- tokens: bfloat16 [8192, 1536], P('dp'), may hold values from -6 to 6
- teacher_feats: bfloat16 [8192, 256], P('dp'), may hold values from -12 to 12
- masks: int32 [32, 256], P('dp'), may hold values from 0 to 1, as said below
- w_in: bfloat16 [1536, 2048], P('dp'), may hold values from -0.15625 to 0.15625
- w_out: bfloat16 [2048, 256], P('dp'), may hold values from -0.125 to 0.125
- proto_student: bfloat16 [256, 131072], P(None, ('dp', 'tensor')), may hold values from -0.375 to 0.375
- proto_teacher: bfloat16 [256, 131072], P(None, ('dp', 'tensor')), may hold values from -1 to 1
Outputs:
- d_tokens: bfloat16 [8192, 1536], P('dp')
- grad_in: float32 [1536, 2048], P('dp')
- grad_out: float32 [2048, 256], P('dp')
- grad_proto: float32 [256, 131072], P(None, ('dp', 'tensor'))
- crop_loss: float32 [32], P('dp')
Inputs may be any that keep to these rules, and one draw needn't show every extreme that they name: `masks`: the crops of one index of dp hold 256 or fewer masked patches together, exactly 256 on some index; a crop holds at most 129.
All inputs are finite; a program needn't handle non-finite values.
Results may differ from a plain program's by a relative error of at most 0.02.
Values may be sent and summed in bfloat16 or wider, within the bound.
A program may use at most 192 MiB of HBM per device.

v0:
```python
import jax
import jax.numpy as jnp
from jax import lax
from jax.sharding import PartitionSpec as P

ROUNDS = 3
CAP = 256


TEACHER_TEMP = 0.07
STUDENT_TEMP = 0.1
EPS = 1e-06
GRAD_SCALE = 65536.0


def gelu_parts(pre):
    cdf = 0.5 * (1.0 + lax.erf(pre * 0.7071067811865476))
    pdf = jnp.exp(-0.5 * pre * pre) * 0.3989422804014327
    return (pre * cdf, cdf + pre * pdf)


def unit_rows(feats):
    inverse = lax.rsqrt(jnp.sum(feats * feats, axis=1, keepdims=True) + EPS)
    return (feats * inverse, inverse)


def unit_columns(protos):
    wide = protos.astype(jnp.float32)
    norms = jnp.sqrt(jnp.sum(wide * wide, axis=0, keepdims=True) + EPS)
    return (wide / norms, norms)


def head_forward(rows, teacher_pick, w_in_all, w_out_all):
    pre = jnp.dot(rows, w_in_all, preferred_element_type=jnp.float32)
    act, slope = gelu_parts(pre)
    hidden = act.astype(jnp.bfloat16)
    feats = jnp.dot(hidden, w_out_all, preferred_element_type=jnp.float32)
    unit, inv = unit_rows(feats)
    teacher_unit, _ = unit_rows(teacher_pick.astype(jnp.float32))
    return (hidden, slope, unit, inv, unit.astype(jnp.bfloat16), teacher_unit.astype(jnp.bfloat16))


def prototype_terms(
    student_rows,
    teacher_rows,
    student_cols,
    teacher_cols,
    live,
    weight,
    col_total,
    row_total,
    last_total,
):
    teacher_cos = jnp.dot(teacher_rows, teacher_cols, preferred_element_type=jnp.float32)
    expo = jnp.exp(teacher_cos / TEACHER_TEMP) * live[:, None]
    scores = jnp.dot(student_rows, student_cols, preferred_element_type=jnp.float32) / STUDENT_TEMP
    raised = jnp.exp(scores)
    scale_row = live
    for turn in range(ROUNDS):
        col_scale = 1.0 / col_total(jnp.sum(expo * scale_row[:, None], axis=0))
        balanced = expo * col_scale[None, :]
        if turn + 1 < ROUNDS:
            row_sum = row_total(jnp.sum(balanced, axis=1))
            scale_row = live / (row_sum + 1.0 - live)
    row_sum, norm_sum, cross = last_total(
        (jnp.sum(balanced, axis=1), jnp.sum(raised, axis=1), jnp.sum(balanced * scores, axis=1))
    )
    scale_row = live / (row_sum + 1.0 - live)
    row_loss = jnp.log(norm_sum) - scale_row * cross
    probs = raised / norm_sum[:, None]
    target = balanced * scale_row[:, None]
    grad_score = (weight[:, None] * (probs - target) / STUDENT_TEMP).astype(jnp.bfloat16)
    grad_part = lax.dot_general(
        grad_score, student_cols, (((1,), (1,)), ((), ())), preferred_element_type=jnp.float32
    )
    return (row_loss, grad_score, grad_part)


def head_backward(rows, hidden, slope, unit, inv, grad_unit, w_in_all, w_out_all):
    inner = jnp.sum(unit * grad_unit, axis=1, keepdims=True)
    grad_feats = (inv * (grad_unit - unit * inner)).astype(jnp.bfloat16)
    grad_out_part = lax.dot_general(
        hidden, grad_feats, (((0,), (0,)), ((), ())), preferred_element_type=jnp.float32
    )
    grad_hidden = lax.dot_general(
        grad_feats, w_out_all, (((1,), (1,)), ((), ())), preferred_element_type=jnp.float32
    )
    grad_pre = (grad_hidden * slope).astype(jnp.bfloat16)
    grad_in_part = lax.dot_general(
        rows, grad_pre, (((0,), (0,)), ((), ())), preferred_element_type=jnp.float32
    )
    grad_rows = lax.dot_general(
        grad_pre, w_in_all, (((1,), (1,)), ((), ())), preferred_element_type=jnp.float32
    )
    return (grad_in_part, grad_out_part, grad_rows)


def shards(tokens, teacher_feats, masks, w_in, w_out, proto_student, proto_teacher):
    crops, patches = masks.shape
    flat = masks.reshape(-1)
    index = jnp.nonzero(flat, size=CAP, fill_value=0)[0].astype(jnp.int32)
    live_own = (jnp.arange(CAP) < jnp.sum(flat)).astype(jnp.float32)
    inverse = 1.0 / jnp.maximum(jnp.sum(masks, axis=1), 1).astype(jnp.float32)
    member = (index[:, None] // patches == jnp.arange(crops)[None, :]).astype(
        jnp.float32
    ) * live_own[:, None]
    weight = (GRAD_SCALE * jnp.sum(member * inverse[None, :], axis=1)).astype(jnp.bfloat16)
    rows = jnp.take(tokens, index, axis=0)
    teacher_pick = jnp.take(teacher_feats, index, axis=0)
    s_cols, s_norm = unit_columns(proto_student)
    t_cols, _ = unit_columns(proto_teacher)
    s_cols_b = s_cols.astype(jnp.bfloat16)
    t_cols_b = t_cols.astype(jnp.bfloat16)
    w_in_all, w_out_all = (
        lax.all_gather(w_in, "dp", axis=0, tiled=True),
        lax.all_gather(w_out, "dp", axis=0, tiled=True),
    )
    hidden, slope, unit, inv, student_rows, teacher_rows = head_forward(
        rows, teacher_pick, w_in_all, w_out_all
    )
    student_every, teacher_every, weight_every = (
        lax.all_gather(student_rows, "dp", axis=0, tiled=True),
        lax.all_gather(teacher_rows, "dp", axis=0, tiled=True),
        lax.all_gather(weight, "dp", axis=0, tiled=True),
    )
    live_every = (weight_every > 0).astype(jnp.float32)

    def col_total(values):
        return values

    def row_total(values):
        return lax.psum(values, ("dp", "tensor"))

    def last_total(values):
        return lax.psum(values, ("dp", "tensor"))

    row_loss_every, grad_score, grad_part = prototype_terms(
        student_every,
        teacher_every,
        s_cols_b,
        t_cols_b,
        live_every,
        weight_every.astype(jnp.float32),
        col_total,
        row_total,
        last_total,
    )
    grad_owned = lax.psum_scatter(grad_part, "dp", scatter_dimension=0, tiled=True)
    grad_unit = lax.psum(grad_owned, "tensor")
    groups = lax.axis_size("dp")
    parts = jnp.einsum(
        "grb,grk->gbk",
        student_every.reshape(groups, CAP, -1),
        grad_score.reshape(groups, CAP, -1),
        preferred_element_type=jnp.float32,
    )
    grad_cols = jnp.sum(
        lax.optimization_barrier(parts.astype(jnp.bfloat16)).astype(jnp.float32), axis=0
    )
    row_loss = lax.dynamic_slice_in_dim(row_loss_every, lax.axis_index("dp") * CAP, CAP)
    grad_in_part, grad_out_part, grad_rows = head_backward(
        rows, hidden, slope, unit, inv, grad_unit, w_in_all, w_out_all
    )
    grad_in, grad_out = (
        lax.psum_scatter(
            grad_in_part.astype(jnp.bfloat16), "dp", scatter_dimension=0, tiled=True
        ).astype(jnp.float32),
        lax.psum_scatter(
            grad_out_part.astype(jnp.bfloat16), "dp", scatter_dimension=0, tiled=True
        ).astype(jnp.float32),
    )
    grad_proto = (grad_cols - s_cols * jnp.sum(s_cols * grad_cols, axis=0, keepdims=True)) / s_norm
    crop_loss = jnp.sum(member * row_loss[:, None], axis=0) * inverse
    placed = (
        jnp.zeros((crops * patches, tokens.shape[1]), jnp.float32)
        .at[index]
        .add(grad_rows * live_own[:, None])
    )
    d_tokens = placed.astype(jnp.bfloat16)
    return (d_tokens, grad_in, grad_out, grad_proto, crop_loss)


def solution(mesh):
    placed = (
        P("dp", None),
        P("dp", None),
        P("dp", None),
        P("dp", None),
        P("dp", None),
        P(None, ("dp", "tensor")),
        P(None, ("dp", "tensor")),
    )
    return jax.shard_map(
        shards,
        mesh=mesh,
        in_specs=placed,
        out_specs=(P("dp", None), P("dp", None), P("dp", None), P(None, ("dp", "tensor")), P("dp")),
        check_vma=False,
    )
```

profile of v0, /device:TPU:1, one launch (start us, length us, event | category | flops | bytes accessed | tf_op | source)
XLA Modules:
  0.0 503.4 jit_solution(13384986147069169513)
XLA Ops:
  10.1 7.6 %scatter_custom_fusion = s32[256]{0:T(256)S(1)} fusion(s32[1024]{0:T(1024)S(1)} %bitcast.39, s32[1024]{0:T(1024)S(1)} %broadcast.305, s32[]{:T(128)} %constant.104.clone.1), kind=kCustom, calls=%fused_computation.100 | custom fusion | flops 1024 | bytes 1028 | tf_op jit(solution)/shard_map/scatter-add | solution.py:101
  25.1 10.3 %all-gather = bf16[8,1,256]{2,1,0:T(2,128)(2,1)S(1)} all-gather(bf16[1,1,256]{2,1,0:T(2,128)(2,1)S(1)} %reshape.285), channel_id=1, replica_groups=mesh['dp'=8,'tensor'=4] {'dp'}, dimensions={0}, use_global_device_ids=true | all-gather | bytes 4608 | tf_op jit(solution)/shard_map/all_gather | solution.py:124
  41.6 7.8 %all-gather.12.cloned.1.call-done = bf16[2048,256]{1,0:T(8,128)(2,1)} async-done(((bf16[256,256]{1,0:T(8,128)(2,1)}), bf16[2048,256]{1,0:T(8,128)(2,1)}) %all-gather.12.cloned.1.call-update) | async-done | bytes 1048592 | tf_op jit(solution)/shard_map/all_gather | solution.py:123
  49.4 17.2 %multiply_reduce_fusion.5 = (f32[4096]{0:T(1024)S(1)}, f32[2048,4096]{1,0:T(8,128)}) fusion(f32[2048]{0:T(1024)S(1)} %bitcast.31, bf16[2048,256]{1,0:T(8,128)(2,1)} %all-gather.12.cloned.1.call-done, bf16[256,4096]{1,0:T(8,128)(2,1)} %param.13, f32[4096]{0:T(1024)S(1)} %add_sqrt_fusion), kind=kOutput, calls=%fused_computation.11 | convolution fusion | flops 4331663360 | bytes 36741120 | tf_op jit(solution)/shard_map/dot_general | solution.py:54
  66.6 13.0 %multiply_reduce_fusion.4 = f32[2048]{0:T(1024)S(1)} fusion(f32[2048,4096]{1,0:T(8,128)} %get-tuple-element.22, f32[4096]{0:T(1024)S(1)} %broadcast_divide_fusion.2), kind=kLoop, calls=%fused_computation.10 | loop fusion | flops 16775168 | bytes 33579008 | tf_op jit(solution)/shard_map/reduce_sum | solution.py:63
  79.7 39.4 %psum.43 = f32[2048]{0:T(1024)S(1)} all-reduce(f32[2048]{0:T(1024)S(1)} %multiply_reduce_fusion.4), channel_id=1, replica_groups=mesh['dp'=8,'tensor'=4] {'dp','tensor'}, use_global_device_ids=true, to_apply=%region_17.18 | all-reduce | flops 2048 | bytes 16384 | tf_op jit(solution)/shard_map/psum | solution.py:132
  119.0 12.9 %multiply_reduce_fusion.3 = f32[4096]{0:T(1024)S(1)} fusion(f32[2048,4096]{1,0:T(8,128)} %get-tuple-element.22, f32[2048]{0:T(1024)S(1)} %subtract_divide_fusion.3), kind=kLoop, calls=%fused_computation.9 | loop fusion | flops 16773120 | bytes 33579008 | tf_op jit(solution)/shard_map/reduce_sum | solution.py:60
  132.0 6.1 %multiply_convert_fusion.1 = (bf16[256,2048]{1,0:T(8,128)(2,1)S(1)}, f32[256,2048]{1,0:T(8,128)}) fusion(bf16[1536,2048]{1,0:T(8,128)(2,1)} %all-gather.6.cloned.1.call-done, bf16[256,1536]{1,0:T(8,128)(2,1)S(1)} %copy-done.3, pred[256]{0:T(512)(128)(4,1)S(1)} %get-tuple-element.14), kind=kOutput, calls=%fused_computation.38 | convolution fusion | flops 1613627392 | bytes 10223872 | tf_op jit(solution)/shard_map/dot_general | solution.py:34
  141.0 12.3 %multiply_reduce_fusion.2 = f32[2048]{0:T(1024)S(1)} fusion(f32[2048,4096]{1,0:T(8,128)} %get-tuple-element.22, f32[4096]{0:T(1024)S(1)} %broadcast_divide_fusion.1), kind=kLoop, calls=%fused_computation.8 | loop fusion | flops 16775168 | bytes 33579008 | tf_op jit(solution)/shard_map/reduce_sum | solution.py:63
  153.3 40.7 %psum.44 = f32[2048]{0:T(1024)S(1)} all-reduce(f32[2048]{0:T(1024)S(1)} %multiply_reduce_fusion.2), channel_id=1, replica_groups=mesh['dp'=8,'tensor'=4] {'dp','tensor'}, use_global_device_ids=true, to_apply=%region_20.21 | all-reduce | flops 2048 | bytes 16384 | tf_op jit(solution)/shard_map/psum | solution.py:132
  194.0 12.9 %multiply_reduce_fusion.1 = f32[4096]{0:T(1024)S(1)} fusion(f32[2048,4096]{1,0:T(8,128)} %get-tuple-element.22, f32[2048]{0:T(1024)S(1)} %subtract_divide_fusion.2), kind=kLoop, calls=%fused_computation.7 | loop fusion | flops 16773120 | bytes 33579008 | tf_op jit(solution)/shard_map/reduce_sum | solution.py:60
  207.0 24.1 %multiply_reduce_fusion = (f32[2048]{0:T(1024)S(1)}, f32[2048]{0:T(1024)S(1)}, f32[2048]{0:T(1024)S(1)}, f32[2048,4096]{1,0:T(8,128)}) fusion(f32[2048,4096]{1,0:T(8,128)} %get-tuple-element.22, f32[4096]{0:T(1024)S(1)} %broadcast_divide_fusion, bf16[2048,256]{0,1:T(8,128)(2,1)} %all-gather.10.cloned.1.call-done, f32[4096]{0:T(1024)S(1)} %add_sqrt_fusion.1, ...), kind=kOutput, calls=%fused_computation.4 | convolution fusion | flops 4348438528 | bytes 70311936 | tf_op jit(solution)/shard_map/dot_general | solution.py:56
  231.1 39.3 %all-reduce = (f32[2048]{0:T(1024)S(1)}, f32[2048]{0:T(1024)S(1)}, f32[2048]{0:T(1024)S(1)}) all-reduce(f32[2048]{0:T(1024)S(1)} %get-tuple-element.6, f32[2048]{0:T(1024)S(1)} %get-tuple-element.7, f32[2048]{0:T(1024)S(1)} %get-tuple-element.5), channel_id=1, replica_groups=mesh['dp'=8,'tensor'=4] {'dp','tensor'}, use_global_device_ids=true, to_apply=%region_23.24 | all-reduce | flops 6144 | bytes 49152 | tf_op jit(solution)/shard_map/psum | solution.py:135
  270.5 27.9 %multiply_convert_fusion = bf16[2048,4096]{1,0:T(8,128)(2,1)} fusion(f32[2048,4096]{1,0:T(8,128)} %get-tuple-element.22, f32[2048,4096]{1,0:T(8,128)} %get-tuple-element.23, f32[2048]{0:T(1024)S(1)} %subtract_divide_fusion.1, f32[4096]{0:T(1024)S(1)} %broadcast_divide_fusion, f32[2048]{0:T(1024)S(1)} %get-tuple-element.12, f32[2048]{0:T(1024)S(1)} %bitcast.35), kind=kLoop, calls=%fused_computation.6 | loop fusion | flops 67108864 | bytes 83927040 | tf_op jit(solution)/shard_map/convert_element_type | solution.py:72
  298.4 9.5 %fusion.28 = f32[2048,256]{0,1:T(8,128)} fusion(bf16[2048,4096]{1,0:T(8,128)(2,1)} %multiply_convert_fusion, f32[4096]{0:T(1024)S(1)} %add_sqrt_fusion.1, bf16[256,4096]{1,0:T(8,128)(2,1)S(1)} %copy-done.2), kind=kOutput, calls=%fused_computation.105 | convolution fusion | flops 4298113024 | bytes 20987904 | tf_op jit(solution)/shard_map/dot_general | solution.py:73
  307.9 42.5 %reduce-scatter.4.cloned.1.call-done = f32[256,256]{0,1:T(8,128)} async-done(((f32[2048,256]{0,1:T(8,128)}), f32[256,256]{0,1:T(8,128)}) %reduce-scatter.4.cloned.1.call-update) | async-done | bytes 262160 | tf_op jit(solution)/shard_map/reduce_scatter | solution.py:148
  350.5 35.8 %all-reduce.3.cloned.1.call-done = f32[256,256]{0,1:T(8,128)} async-done(((f32[256,256]{0,1:T(8,128)}), f32[256,256]{0,1:T(8,128)}) %all-reduce.3.cloned.1.call-update) | async-done | bytes 262160 | tf_op jit(solution)/shard_map/psum | solution.py:149
  395.2 4.6 convolution_convert_fusion.1
  401.0 14.4 %convolution_convert_fusion = bf16[8,256,4096]{2,1,0:T(8,128)(2,1)} fusion(bf16[8,256,4096]{2,1,0:T(8,128)(2,1)} %bitcast.29, bf16[32,8,8,256]{3,2,1,0:T(8,128)(2,1)S(1)} %bitcast.30), kind=kOutput, calls=%fused_computation.15 | convolution fusion | flops 4303355904 | bytes 34603008 | tf_op jit(solution)/shard_map/grb,grk->gbk/dot_general | solution.py:151
  416.1 7.1 %convert_reduce_fusion = f32[256,4096]{1,0:T(8,128)S(1)} fusion(bf16[8,256,4096]{2,1,0:T(8,128)(2,1)} %convolution_convert_fusion), kind=kLoop, calls=%fused_computation.5 | loop fusion | flops 15728640 | bytes 20971520 | tf_op jit(solution)/shard_map/reduce_sum | solution.py:157
  428.1 3.1 convolution_multiply_fusion
  431.2 7.1 %scatter_custom_fusion.1 = f32[1024,1536]{1,0:T(8,128)} fusion(s32[256]{0:T(256)} %bitcast.38, f32[256,1536]{1,0:T(8,128)} %convolution_multiply_fusion, f32[]{:T(128)} %constant.103.clone.1), kind=kCustom, calls=%fused_computation.27 | custom fusion | flops 393216 | bytes 6291968 | tf_op jit(solution)/shard_map/scatter-add | solution.py:177
  438.3 5.2 %convert_element_type.109 = bf16[1024,1536]{1,0:T(8,128)(2,1)} convert(f32[1024,1536]{1,0:T(8,128)} %scatter_custom_fusion.1) | non-fusion elementwise | flops 1572864 | bytes 9437184 | tf_op jit(solution)/shard_map/convert_element_type | solution.py:179
  445.2 49.0 %reduce-scatter.6.cloned.1.call-done = bf16[192,2048]{1,0:T(8,128)(2,1)} async-done(((bf16[1536,2048]{1,0:T(8,128)(2,1)}), bf16[192,2048]{1,0:T(8,128)(2,1)}) %reduce-scatter.6.cloned.1.call-update) | async-done | bytes 786448 | tf_op jit(solution)/shard_map/reduce_scatter | solution.py:165
  (96 shorter events, 39.2 us)
Async XLA Ops:
  7.2 30.3 %copy-start = (bf16[1024,1536]{1,0:T(8,128)(2,1)S(1)}, bf16[1024,1536]{1,0:T(8,128)(2,1)}, u32[]{:S(2)}) copy-start(bf16[1024,1536]{1,0:T(8,128)(2,1)} %param.7) | copy-start | bytes 9437188
  7.2 42.2 %all-gather.12.cloned.1.call-start = ((), (), s32[]{:S(2)}) async-start(), calls=%async_computation.6 | async-start | bytes 1179648 | tf_op jit(solution)/shard_map/all_gather | solution.py:123
  20.3 2.1 copy-start.8
  23.4 108.6 %all-gather.6.cloned.1.call-start = ((), (), s32[]{:S(2)}) async-start(), calls=%async_computation.3 | async-start | bytes 7077888 | tf_op jit(solution)/shard_map/all_gather | solution.py:115
  24.2 113.9 %all-gather.8.cloned.1.call-start = ((), (), s32[]{:S(2)}) async-start(), calls=%async_computation.4 | async-start | bytes 1179648 | tf_op jit(solution)/shard_map/all_gather | solution.py:116
  24.9 182.1 %all-gather.10.cloned.1.call-start = ((), (), s32[]{:S(2)}) async-start(), calls=%async_computation.5 | async-start | bytes 1179648 | tf_op jit(solution)/shard_map/all_gather | solution.py:122
  119.0 13.0 %copy-start.3 = (bf16[256,1536]{1,0:T(8,128)(2,1)S(1)}, bf16[256,1536]{1,0:T(8,128)(2,1)}, u32[]{:S(2)}) copy-start(bf16[256,1536]{1,0:T(8,128)(2,1)} %gather_fusion) | copy-start | bytes 2359300
  138.1 15.2 %copy-start.4 = (bf16[256,2048]{1,0:T(8,128)(2,1)}, bf16[256,2048]{1,0:T(8,128)(2,1)S(1)}, u32[]{:S(2)}) copy-start(bf16[256,2048]{1,0:T(8,128)(2,1)S(1)} %get-tuple-element.17) | copy-start | bytes 3145732
  140.9 209.5 %reduce-scatter.4.cloned.1.call-start = ((), (), s32[]{:S(2)}) async-start(), calls=%async_computation.7 | async-start | bytes 2359296 | tf_op jit(solution)/shard_map/reduce_scatter | solution.py:148
  194.0 13.0 %copy-start.2 = (bf16[256,4096]{1,0:T(8,128)(2,1)S(1)}, bf16[256,4096]{1,0:T(8,128)(2,1)}, u32[]{:S(2)}) copy-start(bf16[256,4096]{1,0:T(8,128)(2,1)} %param.12) | copy-start | bytes 6291460
  307.8 78.5 %all-reduce.3.cloned.1.call-start = ((), (), s32[]{:S(2)}) async-start(), calls=%async_computation.8 | async-start | bytes 524288 | tf_op jit(solution)/shard_map/psum | solution.py:149
  350.4 93.1 %reduce-scatter.8.cloned.1.call-start = ((), (), s32[]{:S(2)}) async-start(), calls=%async_computation.10 | async-start | bytes 1179648 | tf_op jit(solution)/shard_map/reduce_scatter | solution.py:168
  391.1 103.1 %reduce-scatter.6.cloned.1.call-start = ((), (), s32[]{:S(2)}) async-start(), calls=%async_computation.9 | async-start | bytes 7077888 | tf_op jit(solution)/shard_map/reduce_scatter | solution.py:165
  394.2 1.0 copy-start.6
  399.8 1.3 copy-start.5
  423.2 3.8 slice-start
  424.0 3.0 copy-start.7
  424.0 4.0 slice-start.1
  431.2 65.4 %copy-start.1 = (bf16[1024,1536]{1,0:T(8,128)(2,1)S(1)}, bf16[1024,1536]{1,0:T(8,128)(2,1)}, u32[]{:S(2)}) copy-start(bf16[1024,1536]{1,0:T(8,128)(2,1)} %param.7) | copy-start | bytes 9437188
Sparse Core Ops, SparseCore 0:
  23.5 25.8 all-gather.11
  51.3 46.0 all-gather.5
  99.2 23.5 all-gather.7
  141.1 25.4 all-gather.9
  308.0 42.4 reduce-scatter.3
  352.6 33.6 all-reduce.2
  391.2 37.5 reduce-scatter.7
  432.2 61.9 reduce-scatter.5
where the time goes:
time: 505 us; the launch traced here: 503 us
  waiting for transfers between devices  137 us (27%)
  blocking collectives  130 us (26%)
  other arithmetic  128 us (25%)
  matrix products  86.6 us (17%)
  between operations  14.5 us (3%)
  local copies, waits for them, and re-layouts  7.9 us (2%)
    psum x2, blocking collectives, row_total(): return lax.psum(values, ('dp', 'tensor'))  80 us
    reduce_scatter x1, waiting for transfers between devices, shards(): lax.psum_scatter(grad_in_part.astype(jnp.bfloat16), 'dp', scatter_dimensi...  49 us
    reduce_scatter x1, waiting for transfers between devices, shards(): lax.psum_scatter(grad_part, 'dp', scatter_dimension=0, tiled=True)  42.5 us
    psum x1, blocking collectives, last_total(): return lax.psum(values, ('dp', 'tensor'))  39.3 us
    psum x1, waiting for transfers between devices, shards(): grad_unit = lax.psum(grad_owned, 'tensor')  35.8 us
    convert_element_type x1, other arithmetic, prototype_terms(): (weight[:, None] * (probs - target) / STUDENT_TEMP).astype(jnp.bfloat16)  27.9 us
    reduce_sum x2, other arithmetic, prototype_terms(): col_scale = 1.0 / col_total(jnp.sum(expo * scale_row[:, None], axis=0))  25.8 us
    reduce_sum x2, other arithmetic, prototype_terms(): row_sum = row_total(jnp.sum(balanced, axis=1))  25.4 us
  transfers between devices with their start and end apart: 8, of which 4 were waited for; matrix products, arithmetic and copies ran while one was open for 26% of the time, Pallas kernels for 0%

commit v1 on v0

v1 whole, which is shorter than its diff:
```python
import functools

import jax
import jax.numpy as jnp
from jax import lax
from jax.experimental import pallas as pl
from jax.experimental.pallas import tpu as pltpu
from jax.sharding import PartitionSpec as P

ROUNDS = 3
CAP = 256

TEACHER_TEMP = 0.07
STUDENT_TEMP = 0.1
EPS = 1e-06
GRAD_SCALE = 65536.0
LANES = 128
BLOCK = 512
MESH = pl.DeviceIdType.MESH
F32 = jnp.float32
BF16 = jnp.bfloat16


def gelu_parts(pre):
    cdf = 0.5 * (1.0 + lax.erf(pre * 0.7071067811865476))
    pdf = jnp.exp(-0.5 * pre * pre) * 0.3989422804014327
    return (pre * cdf, cdf + pre * pdf)


def unit_rows(feats):
    inverse = lax.rsqrt(jnp.sum(feats * feats, axis=1, keepdims=True) + EPS)
    return (feats * inverse, inverse)


def unit_columns(protos):
    wide = protos.astype(F32)
    norms = jnp.sqrt(jnp.sum(wide * wide, axis=0, keepdims=True) + EPS)
    return (wide / norms, norms)


def spread(dense, out_ref):
    for c in range(dense.shape[0]):
        row = jnp.broadcast_to(dense[c : c + 1, :], (LANES, LANES))
        out_ref[c * LANES : (c + 1) * LANES, :] = row.T


def gathered(acc_ref, out_ref, base):
    for c in range(acc_ref.shape[0] // LANES):
        turned = acc_ref[c * LANES : (c + 1) * LANES, :].T
        out_ref[base + c : base + c + 1, :] = jnp.sum(turned, axis=0, keepdims=True)


def fold_rows(values):
    rows, cols = values.shape
    return jnp.sum(values.reshape(rows // 8, 8, cols), axis=0)


def fold_lanes(values):
    total = values[:, :LANES]
    for start in range(LANES, values.shape[1], LANES):
        total = total + values[:, start : start + LANES]
    return total


def widen(values, cols):
    return jnp.concatenate([values] * (cols // LANES), axis=1)


def chunk(step):
    return pl.ds(pl.multiple_of(step * CAP, CAP), CAP)


def first_kernel(teach, proto, live, expo, sums, live_b, acc):
    rows, block = expo.shape
    here = pl.program_id(0)

    @pl.when(here == 0)
    def _():
        spread(live[...], live_b)
        acc[...] = jnp.zeros_like(acc)

    cols = unit_columns(proto[...])[0].astype(BF16)

    def raise_rows(step, total):
        part = chunk(step)
        cos = jnp.dot(teach[part, :], cols, preferred_element_type=F32)
        value = (jnp.exp(cos * (1.0 / TEACHER_TEMP)) * widen(live_b[part, :], block)).astype(BF16)
        expo[part, :] = value
        return total + fold_rows(value.astype(F32))

    total = lax.fori_loop(0, rows // CAP, raise_rows, jnp.zeros((8, block), F32))
    scale = 1.0 / jnp.sum(total, axis=0, keepdims=True)

    def sum_rows(step, carry):
        part = chunk(step)
        acc[part, :] += fold_lanes(expo[part, :].astype(F32) * scale)
        return carry

    lax.fori_loop(0, rows // CAP, sum_rows, 0)

    @pl.when(here == pl.num_programs(0) - 1)
    def _():
        gathered(acc, sums, 0)


def row_scale(live, row_sum):
    return live / (row_sum + 1.0 - live)


def column_scale(expo, u_b):
    rows, block = expo.shape

    def step_total(step, total):
        part = chunk(step)
        return total + fold_rows(expo[part, :].astype(F32) * widen(u_b[part, :], block))

    total = lax.fori_loop(0, rows // CAP, step_total, jnp.zeros((8, block), F32))
    return 1.0 / jnp.sum(total, axis=0, keepdims=True)


def middle_kernel(expo, live, row_sum, sums, u_b, acc):
    rows, block = expo.shape
    here = pl.program_id(0)

    @pl.when(here == 0)
    def _():
        spread(row_scale(live[...], row_sum[...]), u_b)
        acc[...] = jnp.zeros_like(acc)

    scale = column_scale(expo, u_b)

    def sum_rows(step, carry):
        part = chunk(step)
        acc[part, :] += fold_lanes(expo[part, :].astype(F32) * scale)
        return carry

    lax.fori_loop(0, rows // CAP, sum_rows, 0)

    @pl.when(here == pl.num_programs(0) - 1)
    def _():
        gathered(acc, sums, 0)


def last_kernel(expo, live, row_sum, student, proto, raised, v_out, sums, u_b, acc, acc_n, acc_c):
    rows, block = expo.shape
    here = pl.program_id(0)

    @pl.when(here == 0)
    def _():
        spread(row_scale(live[...], row_sum[...]), u_b)
        acc[...] = jnp.zeros_like(acc)
        acc_n[...] = jnp.zeros_like(acc_n)
        acc_c[...] = jnp.zeros_like(acc_c)

    scale = column_scale(expo, u_b)
    v_out[...] = jnp.broadcast_to(scale, v_out.shape)
    cols = unit_columns(proto[...])[0].astype(BF16)

    def sum_rows(step, carry):
        part = chunk(step)
        scores = jnp.dot(student[part, :], cols, preferred_element_type=F32) * (1.0 / STUDENT_TEMP)
        power = jnp.exp(scores)
        raised[part, :] = power.astype(BF16)
        balanced = expo[part, :].astype(F32) * scale
        acc[part, :] += fold_lanes(balanced)
        acc_n[part, :] += fold_lanes(power)
        acc_c[part, :] += fold_lanes(balanced * scores)
        return carry

    lax.fori_loop(0, rows // CAP, sum_rows, 0)

    @pl.when(here == pl.num_programs(0) - 1)
    def _():
        dense = rows // LANES
        gathered(acc, sums, 0)
        gathered(acc_n, sums, dense)
        gathered(acc_c, sums, 2 * dense)


def grad_kernel(
    expo, raised, v_in, live, weight, sums, student_t, proto, part_out, grad_out, prob_b, target_b, total, cols_total
):
    rows, block = expo.shape
    here = pl.program_id(0)
    dense = rows // LANES

    @pl.when(here == 0)
    def _():
        factor = weight[...] * (1.0 / STUDENT_TEMP)
        spread(factor / sums[dense : 2 * dense, :], prob_b)
        spread(factor * row_scale(live[...], sums[:dense, :]), target_b)
        total[...] = jnp.zeros_like(total)

    unit, norms = unit_columns(proto[...])
    cols = unit.astype(BF16)
    scale = v_in[0:1, :]
    cols_total[...] = jnp.zeros_like(cols_total)

    def one_group(step, carry):
        part = chunk(step)
        target = expo[part, :].astype(F32) * scale * widen(target_b[part, :], block)
        probs = raised[part, :].astype(F32) * widen(prob_b[part, :], block)
        score = (probs - target).astype(BF16)
        total[part, :] += lax.dot_general(
            score, cols, (((1,), (1,)), ((), ())), preferred_element_type=F32
        )
        term = jnp.dot(student_t[:, part], score, preferred_element_type=F32)
        cols_total[...] += term.astype(BF16).astype(F32)
        return carry

    lax.fori_loop(0, rows // CAP, one_group, 0)
    grad = cols_total[...]
    grad_out[...] = (grad - unit * jnp.sum(unit * grad, axis=0, keepdims=True)) / norms

    @pl.when(here == pl.num_programs(0) - 1)
    def _():
        part_out[...] = total[...].astype(BF16)


def whole(shape):
    return pl.BlockSpec(shape, lambda i: tuple(0 for _ in shape))


def tall(rows, block):
    return pl.BlockSpec((rows, block), lambda i: (0, i))


def params(**extra):
    return pltpu.CompilerParams(
        dimension_semantics=("arbitrary",), vmem_limit_bytes=48 * 1024 * 1024, **extra
    )


def cost(flops, moved, powers):
    return pl.CostEstimate(flops=flops, bytes_accessed=moved, transcendentals=powers)


def prototype_first(teach, proto, live):
    rows, width = teach.shape
    columns = proto.shape[1]
    block = min(BLOCK, columns)
    return pl.pallas_call(
        first_kernel,
        name="first_round",
        grid=(columns // block,),
        in_specs=[whole(teach.shape), tall(width, block), whole(live.shape)],
        out_specs=[tall(rows, block), whole(live.shape)],
        out_shape=[jax.ShapeDtypeStruct((rows, columns), BF16), jax.ShapeDtypeStruct(live.shape, F32)],
        scratch_shapes=[pltpu.VMEM((rows, LANES), F32)] * 2,
        compiler_params=params(),
        cost_estimate=cost(2 * rows * width * columns, 2 * rows * columns, rows * columns),
    )(teach, proto, live)


def prototype_middle(expo, live, row_sum):
    rows, columns = expo.shape
    block = min(BLOCK, columns)
    return pl.pallas_call(
        middle_kernel,
        name="middle_round",
        grid=(columns // block,),
        in_specs=[tall(rows, block), whole(live.shape), whole(live.shape)],
        out_specs=whole(live.shape),
        out_shape=jax.ShapeDtypeStruct(live.shape, F32),
        scratch_shapes=[pltpu.VMEM((rows, LANES), F32)] * 2,
        compiler_params=params(),
        cost_estimate=cost(4 * rows * columns, 2 * rows * columns, 0),
    )(expo, live, row_sum)


def prototype_last(expo, live, row_sum, student, proto):
    rows, columns = expo.shape
    width = student.shape[1]
    block = min(BLOCK, columns)
    dense = live.shape[0]
    return pl.pallas_call(
        last_kernel,
        name="last_round",
        grid=(columns // block,),
        in_specs=[
            tall(rows, block),
            whole(live.shape),
            whole(live.shape),
            whole(student.shape),
            tall(width, block),
        ],
        out_specs=[tall(rows, block), tall(8, block), whole((3 * dense, LANES))],
        out_shape=[
            jax.ShapeDtypeStruct((rows, columns), BF16),
            jax.ShapeDtypeStruct((8, columns), F32),
            jax.ShapeDtypeStruct((3 * dense, LANES), F32),
        ],
        scratch_shapes=[pltpu.VMEM((rows, LANES), F32)] * 4,
        compiler_params=params(),
        cost_estimate=cost(2 * rows * width * columns, 4 * rows * columns, rows * columns),
    )(expo, live, row_sum, student, proto)


def prototype_grad(expo, raised, v, live, weight, sums, student_t, proto):
    rows, columns = expo.shape
    width = proto.shape[0]
    block = min(BLOCK, columns)
    return pl.pallas_call(
        grad_kernel,
        name="score_grad",
        grid=(columns // block,),
        in_specs=[
            tall(rows, block),
            tall(rows, block),
            tall(8, block),
            whole(live.shape),
            whole(live.shape),
            whole(sums.shape),
            whole(student_t.shape),
            tall(width, block),
        ],
        out_specs=[whole((rows, width)), tall(width, block)],
        out_shape=[
            jax.ShapeDtypeStruct((rows, width), BF16),
            jax.ShapeDtypeStruct((width, columns), F32),
        ],
        scratch_shapes=[pltpu.VMEM((rows, LANES), F32)] * 2
        + [pltpu.VMEM((rows, width), F32), pltpu.VMEM((width, block), F32)],
        compiler_params=params(),
        cost_estimate=cost(4 * rows * width * columns, 4 * rows * columns, 0),
    )(expo, raised, v, live, weight, sums, student_t, proto)


def greet(groups, many):
    barrier = pltpu.get_barrier_semaphore()
    for axis in ("dp", "tensor"):
        me = lax.axis_index(axis)
        for step in range(1, groups[axis]):
            peer = lax.rem(me + step, groups[axis])
            pl.semaphore_signal(barrier, inc=1, device_id={axis: peer}, device_id_type=MESH)
    pl.semaphore_wait(barrier, many)


def exchange(axis, n, source, landing, send, recv):
    me = lax.axis_index(axis)

    def copy(peer, slot):
        return pltpu.make_async_remote_copy(
            src_ref=source(peer),
            dst_ref=landing.at[slot],
            send_sem=send.at[peer],
            recv_sem=recv.at[slot],
            device_id={axis: peer},
            device_id_type=MESH,
        )

    for step in range(1, n):
        copy(lax.rem(me + step, n), me).start()
    for step in range(1, n):
        peer = lax.rem(me + step, n)
        copy(peer, peer).wait()


def total_kernel(groups, value, out, near, far, send_a, recv_a, send_b, recv_b):
    n, m = groups["dp"], groups["tensor"]
    greet(groups, n + m - 2)
    exchange("dp", n, lambda peer: value, near, send_a, recv_a)
    near[lax.axis_index("dp")] = value[...]
    part = near[0]
    for slot in range(1, n):
        part = part + near[slot]
    out[...] = part
    exchange("tensor", m, lambda peer: out, far, send_b, recv_b)
    far[lax.axis_index("tensor")] = part
    part = far[0]
    for slot in range(1, m):
        part = part + far[slot]
    out[...] = part


def everywhere_total(value, groups, ident):
    n, m = groups["dp"], groups["tensor"]
    return pl.pallas_call(
        functools.partial(total_kernel, groups),
        name=f"row_total_{ident}",
        in_specs=[pl.BlockSpec(memory_space=pltpu.VMEM)],
        out_specs=pl.BlockSpec(memory_space=pltpu.VMEM),
        out_shape=jax.ShapeDtypeStruct(value.shape, F32),
        scratch_shapes=[
            pltpu.VMEM((n,) + value.shape, F32),
            pltpu.VMEM((m,) + value.shape, F32),
            pltpu.SemaphoreType.DMA((n,)),
            pltpu.SemaphoreType.DMA((n,)),
            pltpu.SemaphoreType.DMA((m,)),
            pltpu.SemaphoreType.DMA((m,)),
        ],
        compiler_params=pltpu.CompilerParams(collective_id=ident, has_side_effects=True),
    )(value)


def owner_kernel(groups, value, out, near, far, part, send_a, recv_a, send_b, recv_b):
    n, m = groups["dp"], groups["tensor"]
    greet(groups, n + m - 2)
    me = lax.axis_index("dp")
    exchange("dp", n, lambda peer: value.at[peer], near, send_a, recv_a)
    near[me] = value[me]
    total = near[0].astype(F32)
    for slot in range(1, n):
        total = total + near[slot].astype(F32)
    part[...] = total.astype(BF16)
    exchange("tensor", m, lambda peer: part, far, send_b, recv_b)
    far[lax.axis_index("tensor")] = part[...]
    total = far[0].astype(F32)
    for slot in range(1, m):
        total = total + far[slot].astype(F32)
    out[...] = total


def owner_total(value, groups, ident):
    n, m = groups["dp"], groups["tensor"]
    own = value.shape[1:]
    return pl.pallas_call(
        functools.partial(owner_kernel, groups),
        name="owner_total",
        in_specs=[pl.BlockSpec(memory_space=pltpu.VMEM)],
        out_specs=pl.BlockSpec(memory_space=pltpu.VMEM),
        out_shape=jax.ShapeDtypeStruct(own, F32),
        scratch_shapes=[
            pltpu.VMEM((n,) + own, BF16),
            pltpu.VMEM((m,) + own, BF16),
            pltpu.VMEM(own, BF16),
            pltpu.SemaphoreType.DMA((n,)),
            pltpu.SemaphoreType.DMA((n,)),
            pltpu.SemaphoreType.DMA((m,)),
            pltpu.SemaphoreType.DMA((m,)),
        ],
        compiler_params=pltpu.CompilerParams(collective_id=ident, has_side_effects=True),
    )(value)


def head_forward(rows, w_in_all, w_out_all):
    pre = jnp.dot(rows, w_in_all, preferred_element_type=F32)
    act, slope = gelu_parts(pre)
    hidden = act.astype(BF16)
    feats = jnp.dot(hidden, w_out_all, preferred_element_type=F32)
    unit, inv = unit_rows(feats)
    return (hidden, slope, unit, inv, unit.astype(BF16))


def head_backward(rows, hidden, slope, unit, inv, grad_unit, w_in_all, w_out_all):
    inner = jnp.sum(unit * grad_unit, axis=1, keepdims=True)
    grad_feats = (inv * (grad_unit - unit * inner)).astype(BF16)
    grad_out_part = lax.dot_general(
        hidden, grad_feats, (((0,), (0,)), ((), ())), preferred_element_type=F32
    )
    grad_hidden = lax.dot_general(
        grad_feats, w_out_all, (((1,), (1,)), ((), ())), preferred_element_type=F32
    )
    grad_pre = (grad_hidden * slope).astype(BF16)
    grad_in_part = lax.dot_general(
        rows, grad_pre, (((0,), (0,)), ((), ())), preferred_element_type=F32
    )
    grad_rows = lax.dot_general(
        grad_pre, w_in_all, (((1,), (1,)), ((), ())), preferred_element_type=F32
    )
    return (grad_in_part, grad_out_part, grad_rows)


def selection(masks):
    crops, patches = masks.shape
    size = crops * patches
    flat = masks.reshape(1, size)
    before = (
        lax.broadcasted_iota(jnp.int32, (size, size), 0) < lax.broadcasted_iota(jnp.int32, (size, size), 1)
    ).astype(BF16)
    place = jnp.dot(flat.astype(BF16), before, preferred_element_type=F32).astype(jnp.int32)
    slots = lax.broadcasted_iota(jnp.int32, (CAP, size), 0)
    picked = (place == slots) & (flat > 0)
    dead = slots >= jnp.sum(flat)
    first = lax.broadcasted_iota(jnp.int32, (CAP, size), 1) == 0
    return (picked | (dead & first)).astype(BF16), picked.astype(BF16)


def shards(groups, tokens, teacher_feats, masks, w_in, w_out, proto_student, proto_teacher):
    w_in_all = lax.all_gather(w_in, "dp", axis=0, tiled=True)
    w_out_all = lax.all_gather(w_out, "dp", axis=0, tiled=True)
    pick, place = selection(masks)
    counts = jnp.sum(masks, axis=1)
    ends = jnp.sum(
        jnp.where(jnp.arange(counts.shape[0])[:, None] <= jnp.arange(counts.shape[0])[None, :], counts[:, None], 0),
        axis=0,
    )
    slot = jnp.arange(CAP)[:, None]
    member = ((slot >= (ends - counts)[None, :]) & (slot < ends[None, :])).astype(F32)
    inverse = 1.0 / jnp.maximum(counts, 1).astype(F32)
    weight = (GRAD_SCALE * jnp.sum(member * inverse[None, :], axis=1)).astype(BF16)
    teacher_pick = jnp.dot(pick, teacher_feats, preferred_element_type=F32)
    teacher_rows = unit_rows(teacher_pick)[0].astype(BF16)
    teacher_every = lax.all_gather(teacher_rows, "dp", axis=0, tiled=True)
    weight_every = lax.all_gather(weight, "dp", axis=0, tiled=True).astype(F32)
    weight_every = weight_every.reshape(-1, LANES)
    live_every = (weight_every > 0).astype(F32)

    expo, row_sum = prototype_first(teacher_every, proto_teacher, live_every)
    row_sum = everywhere_total(row_sum, groups, 1)

    rows = jnp.dot(pick, tokens, preferred_element_type=F32).astype(BF16)
    hidden, slope, unit, inv, student_rows = head_forward(rows, w_in_all, w_out_all)
    student_every = lax.all_gather(student_rows, "dp", axis=0, tiled=True)

    for turn in range(ROUNDS - 2):
        row_sum = prototype_middle(expo, live_every, row_sum)
        row_sum = everywhere_total(row_sum, groups, 2 + turn)
    raised, v, sums = prototype_last(expo, live_every, row_sum, student_every, proto_student)
    sums = everywhere_total(sums, groups, ROUNDS)
    grad_part, grad_proto = prototype_grad(
        expo, raised, v, live_every, weight_every, sums, student_every.T, proto_student
    )
    grad_unit = owner_total(grad_part.reshape(groups["dp"], CAP, -1), groups, ROUNDS + 1)

    dense = live_every.shape[0]
    own = CAP // LANES
    start = lax.axis_index("dp") * own

    def mine(values):
        return lax.dynamic_slice_in_dim(values, start, own).reshape(CAP)

    live_own = mine(live_every)
    scale_row = live_own / (mine(sums[:dense]) + 1.0 - live_own)
    row_loss = jnp.log(mine(sums[dense : 2 * dense])) - scale_row * mine(sums[2 * dense :])
    crop_loss = jnp.sum(member * row_loss[:, None], axis=0) * inverse

    grad_in_part, grad_out_part, grad_rows = head_backward(
        rows, hidden, slope, unit, inv, grad_unit, w_in_all, w_out_all
    )
    grad_in, grad_out = (
        lax.psum_scatter(grad_in_part.astype(BF16), "dp", scatter_dimension=0, tiled=True).astype(F32),
        lax.psum_scatter(grad_out_part.astype(BF16), "dp", scatter_dimension=0, tiled=True).astype(F32),
    )
    d_tokens = lax.dot_general(
        place, grad_rows.astype(BF16), (((0,), (0,)), ((), ())), preferred_element_type=F32
    ).astype(BF16)
    return (d_tokens, grad_in, grad_out, grad_proto, crop_loss)


def solution(mesh):
    groups = {"dp": mesh.shape["dp"], "tensor": mesh.shape["tensor"]}
    placed = (
        P("dp", None),
        P("dp", None),
        P("dp", None),
        P("dp", None),
        P("dp", None),
        P(None, ("dp", "tensor")),
        P(None, ("dp", "tensor")),
    )
    return jax.shard_map(
        functools.partial(shards, groups),
        mesh=mesh,
        in_specs=placed,
        out_specs=(P("dp", None), P("dp", None), P("dp", None), P(None, ("dp", "tensor")), P("dp")),
        check_vma=False,
    )
```

time: 505 us -> 391 us (0.77)
  Pallas kernels: 0 us -> 157 us
  blocking collectives: 130 us -> 9.01 us
  other arithmetic: 128 us -> 11.6 us
  matrix products: 86.6 us -> 31.5 us
  waiting for transfers between devices: 137 us -> 154 us
    pallas_call x0 -> x8, Pallas kernels: none -> 157 us  [the longest x3 32.3 us: everywhere_total(): pl.pallas_call(functools.partial(total_kernel, groups), name=f'row_total_...]
    psum x3 -> x0, blocking collectives: 119 us -> none  [the longest x2 80 us: row_total(): return lax.psum(values, ('dp', 'tensor'))]
    reduce_sum x10 -> x2, other arithmetic: 64.7 us -> 1.51 us  [the longest x1 1.43 us: shards(): counts = jnp.sum(masks, axis=1)]
    all_gather x4, waiting for transfers between devices: 7.82 us -> 70.9 us  [the longest x1 39.7 us: shards(): w_in_all = lax.all_gather(w_in, 'dp', axis=0, tiled=True)]
    dot_general x7 -> x6, matrix products: 76.5 us -> 21 us  [the longest x1 7.71 us: shards(): lax.dot_general(place, grad_rows.astype(BF16), (((0,), (0,)), ((), ())),...]
    psum x1 -> x0, waiting for transfers between devices: 35.8 us -> none  [shards(): grad_unit = lax.psum(grad_owned, 'tensor')]
    convert_element_type x11 -> x8, other arithmetic: 40.5 us -> 6.79 us  [the longest x1 2.45 us: shards(): lax.psum_scatter(grad_in_part.astype(BF16), 'dp', scatter_dimension=0, ti...]
    scatter-add x2 -> x0, other arithmetic: 14.7 us -> none  [the longest x1 7.61 us: shards(): index = jnp.nonzero(flat, size=CAP, fill_value=0)[0].astype(jnp.int32)]
  transfers between devices with their start and end apart: 8 -> 6, of which waited for: 4 -> 5; matrix products, arithmetic and copies ran while one was open for 26% -> 10% of each run, Pallas kernels for 0% -> 15%
where the time goes in v1:
time: 391 us; the launch traced here: 389 us
  Pallas kernels  157 us (40%)
  waiting for transfers between devices  154 us (39%)
  matrix products  31.5 us (8%)
  between operations  14.4 us (4%)
  other arithmetic  11.6 us (3%)
  local copies, waits for them, and re-layouts  11.5 us (3%)
  blocking collectives  9.01 us (2%)
    reduce_scatter x1, waiting for transfers between devices, shards(): lax.psum_scatter(grad_in_part.astype(BF16), 'dp', scatter_dimension=0, ti...  63.6 us
    all_gather x1, waiting for transfers between devices, shards(): w_in_all = lax.all_gather(w_in, 'dp', axis=0, tiled=True)  39.7 us
    pallas_call x3, Pallas kernels, everywhere_total(): pl.pallas_call(functools.partial(total_kernel, groups), name=f'row_total_...  32.3 us
    pallas_call x1, Pallas kernels, prototype_last(): pl.pallas_call(last_kernel, name='last_round', grid=(columns // block,),...  29 us
    pallas_call x1, Pallas kernels, owner_total(): pl.pallas_call(functools.partial(owner_kernel, groups), name='owner_total...  28.7 us
    pallas_call x1, Pallas kernels, prototype_grad(): pl.pallas_call(grad_kernel, name='score_grad', grid=(columns // block,),...  28.1 us
    pallas_call x1, Pallas kernels, prototype_first(): pl.pallas_call(first_kernel, name='first_round', grid=(columns // block,)...  25.7 us
    all_gather x1, waiting for transfers between devices, shards(): w_out_all = lax.all_gather(w_out, 'dp', axis=0, tiled=True)  19 us
  transfers between devices with their start and end apart: 6, of which 5 were waited for; matrix products, arithmetic and copies ran while one was open for 10% of the time, Pallas kernels for 15%

profile of v1, /device:TPU:1, one launch (start us, length us, event | category | flops | bytes accessed | tf_op | source)
XLA Modules:
  0.0 389.2 jit_solution(15793297590855356897)
XLA Ops:
  11.8 2.3 multiply_reduce_fusion.1
  16.1 2.0 convolution_convert_fusion.4
  18.1 39.7 %all-gather.6.cloned.1.call-done = bf16[1536,2048]{1,0:T(8,128)(2,1)} async-done(((bf16[192,2048]{1,0:T(8,128)(2,1)}), bf16[1536,2048]{1,0:T(8,128)(2,1)}) %all-gather.6.cloned.1.call-update) | async-done | bytes 6291472 | tf_op jit(solution)/shard_map/all_gather | solution.py:480
  57.8 6.3 %multiply_convert_fusion = (bf16[256,2048]{1,0:T(8,128)(2,1)S(1)}, f32[256,2048]{1,0:T(8,128)}) fusion(bf16[256,1536]{1,0:T(8,128)(2,1)} %convolution_convert_fusion.4, bf16[1536,2048]{1,0:T(8,128)(2,1)} %all-gather.6.cloned.1.call-done), kind=kOutput, calls=%fused_computation.14 | convolution fusion | flops 1613234176 | bytes 10223616 | tf_op jit(solution)/shard_map/dot_general | solution.py:437
  64.1 19.0 %all-gather.8.cloned.1.call-done = bf16[2048,256]{1,0:T(8,128)(2,1)} async-done(((bf16[256,256]{1,0:T(8,128)(2,1)}), bf16[2048,256]{1,0:T(8,128)(2,1)}) %all-gather.8.cloned.1.call-update) | async-done | bytes 1048592 | tf_op jit(solution)/shard_map/all_gather | solution.py:481
  83.0 2.5 multiply_reduce_fusion.2
  87.7 9.0 %all-gather = bf16[8,1,256]{2,1,0:T(2,128)(2,1)S(1)} all-gather(bf16[1,1,256]{2,1,0:T(2,128)(2,1)S(1)} %reshape.106), channel_id=1, replica_groups=mesh['dp'=8,'tensor'=4] {'dp'}, dimensions={0}, use_global_device_ids=true | all-gather | bytes 4608 | tf_op jit(solution)/shard_map/all_gather | solution.py:495
  96.7 12.2 %all-gather.10.cloned.1.call-done.teach = bf16[2048,256]{1,0:T(8,128)(2,1)} async-done(((bf16[256,256]{1,0:T(8,128)(2,1)}), bf16[2048,256]{1,0:T(8,128)(2,1)}) %all-gather.10.cloned.1.call-update) | async-done | bytes 1048592 | tf_op jit(solution)/shard_map/all_gather | solution.py:494
  110.1 25.7 %first_round.1 = (bf16[2048,4096]{1,0:T(8,128)(2,1)}, f32[16,128]{1,0:T(8,128)S(1)}) custom-call(bf16[2048,256]{1,0:T(8,128)(2,1)S(1)} %copy-done.14, bf16[256,4096]{1,0:T(8,128)(2,1)S(1)} %copy-done.13, f32[16,128]{1,0:T(8,128)S(1)} %compare_convert_fusion.live), custom_call_target="tpu_custom_call" | custom-call | flops 4294967296 | bytes 16777216 | tf_op jit(solution)/shard_map/first_round/pallas_call | solution.py:242
  136.4 10.3 %row_total_1.1.row_sum = f32[16,128]{1,0:T(8,128)} custom-call(f32[16,128]{1,0:T(8,128)} %copy-done.12), custom_call_target="tpu_custom_call" | custom-call | tf_op jit(solution)/shard_map/row_total_1/pallas_call | solution.py:378
  147.4 12.7 %middle_round.1.value = f32[16,128]{1,0:T(8,128)S(1)} custom-call(bf16[2048,4096]{1,0:T(8,128)(2,1)} %get-tuple-element.12.expo, f32[16,128]{1,0:T(8,128)S(1)} %compare_convert_fusion.live, f32[16,128]{1,0:T(8,128)S(1)} %copy-done.9), custom_call_target="tpu_custom_call" | custom-call | flops 33554432 | bytes 16777216 | tf_op jit(solution)/shard_map/middle_round/pallas_call | solution.py:258
  160.7 10.4 %row_total_2.1.row_sum = f32[16,128]{1,0:T(8,128)} custom-call(f32[16,128]{1,0:T(8,128)} %copy-done.10), custom_call_target="tpu_custom_call" | custom-call | tf_op jit(solution)/shard_map/row_total_2/pallas_call | solution.py:378
  173.1 29.0 %last_round.1 = (bf16[2048,4096]{1,0:T(8,128)(2,1)}, f32[8,4096]{1,0:T(8,128)S(1)}, f32[48,128]{1,0:T(8,128)S(1)}) custom-call(bf16[2048,4096]{1,0:T(8,128)(2,1)} %get-tuple-element.12.expo, f32[16,128]{1,0:T(8,128)S(1)} %compare_convert_fusion.live, f32[16,128]{1,0:T(8,128)S(1)} %copy-done.8, bf16[2048,256]{1,0:T(8,128)(2,1)S(1)} %copy-done.3, ...), custom_call_target="tpu_custom_call" | custom-call | flops 4294967296 | bytes 33554432 | tf_op jit(solution)/shard_map/last_round/pallas_call | solution.py:276
  202.7 11.6 %row_total_3.1.sums = f32[48,128]{1,0:T(8,128)} custom-call(f32[48,128]{1,0:T(8,128)} %copy-done.11), custom_call_target="tpu_custom_call" | custom-call | tf_op jit(solution)/shard_map/row_total_3/pallas_call | solution.py:378
  217.0 28.1 %score_grad.1 = (bf16[2048,256]{1,0:T(8,128)(2,1)S(1)}, f32[256,4096]{1,0:T(8,128)}) custom-call(bf16[2048,4096]{1,0:T(8,128)(2,1)} %get-tuple-element.12.expo, bf16[2048,4096]{1,0:T(8,128)(2,1)} %get-tuple-element.14.raised, f32[8,4096]{1,0:T(8,128)S(1)} %get-tuple-element.15.v_in, f32[16,128]{1,0:T(8,128)S(1)} %compare_convert_fusion.live, ...), custom_call_target="tpu_custom_call" | custom-call | flops 8589934592 | bytes 33554432 | tf_op jit(solution)/shard_map/score_grad/pallas_call | solution.py:303
  246.1 28.7 %owner_total.1 = f32[256,256]{1,0:T(8,128)} custom-call(bf16[8,256,256]{2,1,0:T(8,128)(2,1)} %bitcast.39), custom_call_target="tpu_custom_call" | custom-call | tf_op jit(solution)/shard_map/owner_total/pallas_call | solution.py:417
  277.2 1.5 convolution_convert_fusion.2
  279.0 3.2 fusion.1
  282.2 5.7 %convolution_convert_fusion = bf16[1536,2048]{1,0:T(8,128)(2,1)} fusion(bf16[256,1536]{1,0:T(8,128)(2,1)S(1)} %copy-done.19, bf16[256,2048]{1,0:T(8,128)(2,1)} %fusion.1), kind=kOutput, calls=%fused_computation | convolution fusion | flops 1613758464 | bytes 8126464 | tf_op jit(solution)/shard_map/dot_general | solution.py:455
  288.7 7.7 %convolution_convert_fusion.1 = bf16[1024,1536]{1,0:T(8,128)(2,1)} fusion(bf16[256,2048]{1,0:T(8,128)(2,1)} %fusion.1, bf16[1536,2048]{1,0:T(8,128)(2,1)} %all-gather.6.cloned.1.call-done, s32[1024]{0:T(1024)S(1)} %convert_element_type.69, pred[1024]{0:T(1024)(128)(4,1)S(1)} %gt.24), kind=kOutput, calls=%fused_computation.3 | convolution fusion | flops 2418409472 | bytes 10490880 | tf_op jit(solution)/shard_map/dot_general | solution.py:535
  296.4 18.2 %reduce-scatter.5.cloned.1.call-done = bf16[256,256]{1,0:T(8,128)(2,1)} async-done(((bf16[2048,256]{1,0:T(8,128)(2,1)}), bf16[256,256]{1,0:T(8,128)(2,1)}) %reduce-scatter.5.cloned.1.call-update) | async-done | bytes 131088 | tf_op jit(solution)/shard_map/reduce_scatter | solution.py:533
  314.7 1.6 convert_element_type.84
  316.3 63.6 %reduce-scatter.3.cloned.1.call-done = bf16[192,2048]{1,0:T(8,128)(2,1)} async-done(((bf16[1536,2048]{1,0:T(8,128)(2,1)}), bf16[192,2048]{1,0:T(8,128)(2,1)}) %reduce-scatter.3.cloned.1.call-update) | async-done | bytes 786448 | tf_op jit(solution)/shard_map/reduce_scatter | solution.py:532
  379.9 2.5 convert_element_type.82
  (84 shorter events, 21.2 us)
Async XLA Ops:
  7.2 8.9 %copy-start = (bf16[1024,1536]{1,0:T(8,128)(2,1)S(1)}, bf16[1024,1536]{1,0:T(8,128)(2,1)}, u32[]{:S(2)}) copy-start(bf16[1024,1536]{1,0:T(8,128)(2,1)} %param.7) | copy-start | bytes 9437188
  7.2 50.6 %all-gather.6.cloned.1.call-start = ((), (), s32[]{:S(2)}) async-start(), calls=%async_computation.2 | async-start | bytes 7077888 | tf_op jit(solution)/shard_map/all_gather | solution.py:480
  7.9 75.1 %all-gather.8.cloned.1.call-start = ((), (), s32[]{:S(2)}) async-start(), calls=%async_computation.3 | async-start | bytes 1179648 | tf_op jit(solution)/shard_map/all_gather | solution.py:481
  8.7 100.2 %all-gather.10.cloned.1.call-start = ((), (), s32[]{:S(2)}) async-start(), calls=%async_computation.4 | async-start | bytes 1179648 | tf_op jit(solution)/shard_map/all_gather | solution.py:494
  16.0 155.1 %all-gather.12.cloned.1.call-start = ((), (), s32[]{:S(2)}) async-start(), calls=%async_computation.5 | async-start | bytes 1179648 | tf_op jit(solution)/shard_map/all_gather | solution.py:504
  64.1 32.6 %copy-start.15 = (bf16[256,2048]{1,0:T(8,128)(2,1)}, bf16[256,2048]{1,0:T(8,128)(2,1)S(1)}, u32[]{:S(2)}) copy-start(bf16[256,2048]{1,0:T(8,128)(2,1)S(1)} %get-tuple-element.27) | copy-start | bytes 3145732
  64.1 44.8 %copy-start.13 = (bf16[256,4096]{1,0:T(8,128)(2,1)S(1)}, bf16[256,4096]{1,0:T(8,128)(2,1)}, u32[]{:S(2)}) copy-start(bf16[256,4096]{1,0:T(8,128)(2,1)} %proto.3) | copy-start | bytes 6291460
  86.6 1.1 copy-start.17
  87.4 227.3 %reduce-scatter.5.cloned.1.call-start = ((), (), s32[]{:S(2)}) async-start(), calls=%async_computation.7 | async-start | bytes 1179648 | tf_op jit(solution)/shard_map/reduce_scatter | solution.py:533
  108.9 1.2 copy-start.14
  146.7 0.7 copy-start.9
  147.4 23.7 %copy-start.2 = (bf16[256,4096]{1,0:T(8,128)(2,1)S(1)}, bf16[256,4096]{1,0:T(8,128)(2,1)}, u32[]{:S(2)}) copy-start(bf16[256,4096]{1,0:T(8,128)(2,1)} %proto.5) | copy-start | bytes 6291460
  171.1 1.2 copy-start.3
  172.4 0.7 copy-start.8
  173.1 41.3 %copy-start.4 = (bf16[2048,256]{1,0:T(8,128)(2,1)S(1)}, bf16[2048,256]{1,0:T(8,128)(2,1)}, u32[]{:S(2)}) copy-start(bf16[2048,256]{1,0:T(8,128)(2,1)} %all-gather.12.cloned.1.call-done.student) | copy-start | bytes 3145732
  214.3 1.4 copy-start.7
  215.8 1.2 copy-start.5
  217.0 57.8 %copy-start.18 = (f32[256,256]{1,0:T(8,128)S(1)}, f32[256,256]{1,0:T(8,128)}, u32[]{:S(2)}) copy-start(f32[256,256]{1,0:T(8,128)} %copy-done.17) | copy-start | bytes 786436
  245.1 1.0 copy-start.6
  246.1 31.1 %copy-start.16 = (bf16[256,2048]{1,0:T(8,128)(2,1)S(1)}, bf16[256,2048]{1,0:T(8,128)(2,1)}, u32[]{:S(2)}) copy-start(bf16[256,2048]{1,0:T(8,128)(2,1)} %copy-done.15) | copy-start | bytes 3145732
  276.0 2.9 copy-start.20
  278.7 101.2 %reduce-scatter.3.cloned.1.call-start = ((), (), s32[]{:S(2)}) async-start(), calls=%async_computation.6 | async-start | bytes 7077888 | tf_op jit(solution)/shard_map/reduce_scatter | solution.py:532
  278.9 3.2 copy-start.19
  288.7 93.7 %copy-start.1 = (bf16[1024,1536]{1,0:T(8,128)(2,1)S(1)}, bf16[1024,1536]{1,0:T(8,128)(2,1)}, u32[]{:S(2)}) copy-start(bf16[1024,1536]{1,0:T(8,128)(2,1)} %param.7) | copy-start | bytes 9437188
  (3 other events, 1.8 us)
Sparse Core Ops, SparseCore 0:
  9.9 47.8 all-gather.5
  59.7 23.3 all-gather.7
  85.5 23.3 all-gather.9
  111.2 23.3 all-gather.11
  278.8 35.7 reduce-scatter.4
  317.9 61.9 reduce-scatter.2

commit v2 on v1

--- a/solution.py
+++ b/solution.py
@@ -14,6 +14,7 @@
 STUDENT_TEMP = 0.1
 EPS = 1e-06
 GRAD_SCALE = 65536.0
+LOG2E = 1.4426950408889634
 LANES = 128
 BLOCK = 512
 MESH = pl.DeviceIdType.MESH
@@ -50,11 +51,6 @@
         out_ref[base + c : base + c + 1, :] = jnp.sum(turned, axis=0, keepdims=True)
 
 
-def fold_rows(values):
-    rows, cols = values.shape
-    return jnp.sum(values.reshape(rows // 8, 8, cols), axis=0)
-
-
 def fold_lanes(values):
     total = values[:, :LANES]
     for start in range(LANES, values.shape[1], LANES):
@@ -70,101 +66,102 @@
     return pl.ds(pl.multiple_of(step * CAP, CAP), CAP)
 
 
-def first_kernel(teach, proto, live, expo, sums, live_b, acc):
+def two_terms(row):
+    high = row.astype(BF16)
+    low = (row - high.astype(F32)).astype(BF16)
+    return jnp.concatenate([high, low, jnp.zeros((14, row.shape[1]), BF16)], axis=0)
+
+
+def flatten(dense):
+    return jnp.concatenate([dense[c : c + 1, :] for c in range(dense.shape[0])], axis=1)
+
+
+def row_scale(live, row_sum):
+    return live / (row_sum + 1.0 - live)
+
+
+def column_scale(expo, u_terms):
+    total = jnp.dot(u_terms[...], expo[...], preferred_element_type=F32)
+    return 1.0 / (total[0:1, :] + total[1:2, :])
+
+
+def add_row_sums(expo, scale, acc):
+    terms = two_terms(scale)
+
+    def sum_rows(step, carry):
+        part = chunk(step)
+        acc[part, :] += lax.dot_general(
+            expo[part, :], terms, (((1,), (1,)), ((), ())), preferred_element_type=F32
+        )
+        return carry
+
+    lax.fori_loop(0, expo.shape[0] // CAP, sum_rows, 0)
+
+
+def first_kernel(teach, proto, live, expo, sums, u_terms, acc):
     rows, block = expo.shape
     here = pl.program_id(0)
 
     @pl.when(here == 0)
     def _():
-        spread(live[...], live_b)
+        u_terms[...] = two_terms(flatten(live[...]))
         acc[...] = jnp.zeros_like(acc)
 
     cols = unit_columns(proto[...])[0].astype(BF16)
 
-    def raise_rows(step, total):
+    def raise_rows(step, carry):
         part = chunk(step)
         cos = jnp.dot(teach[part, :], cols, preferred_element_type=F32)
-        value = (jnp.exp(cos * (1.0 / TEACHER_TEMP)) * widen(live_b[part, :], block)).astype(BF16)
-        expo[part, :] = value
-        return total + fold_rows(value.astype(F32))
-
-    total = lax.fori_loop(0, rows // CAP, raise_rows, jnp.zeros((8, block), F32))
-    scale = 1.0 / jnp.sum(total, axis=0, keepdims=True)
-
-    def sum_rows(step, carry):
-        part = chunk(step)
-        acc[part, :] += fold_lanes(expo[part, :].astype(F32) * scale)
+        expo[part, :] = jnp.exp2(cos * (LOG2E / TEACHER_TEMP)).astype(BF16)
         return carry
 
-    lax.fori_loop(0, rows // CAP, sum_rows, 0)
+    lax.fori_loop(0, rows // CAP, raise_rows, 0)
+    add_row_sums(expo, column_scale(expo, u_terms), acc)
 
     @pl.when(here == pl.num_programs(0) - 1)
     def _():
         gathered(acc, sums, 0)
 
 
-def row_scale(live, row_sum):
-    return live / (row_sum + 1.0 - live)
-
-
-def column_scale(expo, u_b):
-    rows, block = expo.shape
-
-    def step_total(step, total):
-        part = chunk(step)
-        return total + fold_rows(expo[part, :].astype(F32) * widen(u_b[part, :], block))
-
-    total = lax.fori_loop(0, rows // CAP, step_total, jnp.zeros((8, block), F32))
-    return 1.0 / jnp.sum(total, axis=0, keepdims=True)
-
-
-def middle_kernel(expo, live, row_sum, sums, u_b, acc):
+def middle_kernel(expo, live, row_sum, sums, u_terms, acc):
+    here = pl.program_id(0)
+
+    @pl.when(here == 0)
+    def _():
+        u_terms[...] = two_terms(flatten(row_scale(live[...], row_sum[...])))
+        acc[...] = jnp.zeros_like(acc)
+
+    add_row_sums(expo, column_scale(expo, u_terms), acc)
+
+    @pl.when(here == pl.num_programs(0) - 1)
+    def _():
+        gathered(acc, sums, 0)
+
+
+def last_kernel(expo, live, row_sum, student, proto, raised, v_out, sums, u_terms, acc, acc_n, acc_c):
     rows, block = expo.shape
     here = pl.program_id(0)
 
     @pl.when(here == 0)
     def _():
-        spread(row_scale(live[...], row_sum[...]), u_b)
-        acc[...] = jnp.zeros_like(acc)
-
-    scale = column_scale(expo, u_b)
-
-    def sum_rows(step, carry):
-        part = chunk(step)
-        acc[part, :] += fold_lanes(expo[part, :].astype(F32) * scale)
-        return carry
-
-    lax.fori_loop(0, rows // CAP, sum_rows, 0)
-
-    @pl.when(here == pl.num_programs(0) - 1)
-    def _():
-        gathered(acc, sums, 0)
-
-
-def last_kernel(expo, live, row_sum, student, proto, raised, v_out, sums, u_b, acc, acc_n, acc_c):
-    rows, block = expo.shape
-    here = pl.program_id(0)
-
-    @pl.when(here == 0)
-    def _():
-        spread(row_scale(live[...], row_sum[...]), u_b)
+        u_terms[...] = two_terms(flatten(row_scale(live[...], row_sum[...])))
         acc[...] = jnp.zeros_like(acc)
         acc_n[...] = jnp.zeros_like(acc_n)
         acc_c[...] = jnp.zeros_like(acc_c)
 
-    scale = column_scale(expo, u_b)
+    scale = column_scale(expo, u_terms)
     v_out[...] = jnp.broadcast_to(scale, v_out.shape)
     cols = unit_columns(proto[...])[0].astype(BF16)
 
     def sum_rows(step, carry):
         part = chunk(step)
-        scores = jnp.dot(student[part, :], cols, preferred_element_type=F32) * (1.0 / STUDENT_TEMP)
-        power = jnp.exp(scores)
+        dots = jnp.dot(student[part, :], cols, preferred_element_type=F32)
+        power = jnp.exp2(dots * (LOG2E / STUDENT_TEMP))
         raised[part, :] = power.astype(BF16)
         balanced = expo[part, :].astype(F32) * scale
         acc[part, :] += fold_lanes(balanced)
         acc_n[part, :] += fold_lanes(power)
-        acc_c[part, :] += fold_lanes(balanced * scores)
+        acc_c[part, :] += fold_lanes(balanced * dots)
         return carry
 
     lax.fori_loop(0, rows // CAP, sum_rows, 0)
@@ -172,13 +169,14 @@
     @pl.when(here == pl.num_programs(0) - 1)
     def _():
         dense = rows // LANES
+        acc_c[...] = acc_c[...] * (1.0 / STUDENT_TEMP)
         gathered(acc, sums, 0)
         gathered(acc_n, sums, dense)
         gathered(acc_c, sums, 2 * dense)
 
 
 def grad_kernel(
-    expo, raised, v_in, live, weight, sums, student_t, proto, part_out, grad_out, prob_b, target_b, total, cols_total
+    expo, raised, v_in, live, weight, sums, student_t, proto, part_out, grad_out, prob_b, target_b, total, score
 ):
     rows, block = expo.shape
     here = pl.program_id(0)
@@ -194,22 +192,20 @@
     unit, norms = unit_columns(proto[...])
     cols = unit.astype(BF16)
     scale = v_in[0:1, :]
-    cols_total[...] = jnp.zeros_like(cols_total)
 
     def one_group(step, carry):
         part = chunk(step)
         target = expo[part, :].astype(F32) * scale * widen(target_b[part, :], block)
         probs = raised[part, :].astype(F32) * widen(prob_b[part, :], block)
-        score = (probs - target).astype(BF16)
+        value = (probs - target).astype(BF16)
+        score[part, :] = value
         total[part, :] += lax.dot_general(
-            score, cols, (((1,), (1,)), ((), ())), preferred_element_type=F32
-        )
-        term = jnp.dot(student_t[:, part], score, preferred_element_type=F32)
-        cols_total[...] += term.astype(BF16).astype(F32)
+            value, cols, (((1,), (1,)), ((), ())), preferred_element_type=F32
+        )
         return carry
 
     lax.fori_loop(0, rows // CAP, one_group, 0)
-    grad = cols_total[...]
+    grad = jnp.dot(student_t[...], score[...], preferred_element_type=F32)
     grad_out[...] = (grad - unit * jnp.sum(unit * grad, axis=0, keepdims=True)) / norms
 
     @pl.when(here == pl.num_programs(0) - 1)
@@ -246,7 +242,7 @@
         in_specs=[whole(teach.shape), tall(width, block), whole(live.shape)],
         out_specs=[tall(rows, block), whole(live.shape)],
         out_shape=[jax.ShapeDtypeStruct((rows, columns), BF16), jax.ShapeDtypeStruct(live.shape, F32)],
-        scratch_shapes=[pltpu.VMEM((rows, LANES), F32)] * 2,
+        scratch_shapes=[pltpu.VMEM((16, rows), BF16), pltpu.VMEM((rows, 16), F32)],
         compiler_params=params(),
         cost_estimate=cost(2 * rows * width * columns, 2 * rows * columns, rows * columns),
     )(teach, proto, live)
@@ -262,7 +258,7 @@
         in_specs=[tall(rows, block), whole(live.shape), whole(live.shape)],
         out_specs=whole(live.shape),
         out_shape=jax.ShapeDtypeStruct(live.shape, F32),
-        scratch_shapes=[pltpu.VMEM((rows, LANES), F32)] * 2,
+        scratch_shapes=[pltpu.VMEM((16, rows), BF16), pltpu.VMEM((rows, 16), F32)],
         compiler_params=params(),
         cost_estimate=cost(4 * rows * columns, 2 * rows * columns, 0),
     )(expo, live, row_sum)
@@ -290,7 +286,7 @@
             jax.ShapeDtypeStruct((8, columns), F32),
             jax.ShapeDtypeStruct((3 * dense, LANES), F32),
         ],
-        scratch_shapes=[pltpu.VMEM((rows, LANES), F32)] * 4,
+        scratch_shapes=[pltpu.VMEM((16, rows), BF16)] + [pltpu.VMEM((rows, LANES), F32)] * 3,
         compiler_params=params(),
         cost_estimate=cost(2 * rows * width * columns, 4 * rows * columns, rows * columns),
     )(expo, live, row_sum, student, proto)
@@ -320,7 +316,7 @@
             jax.ShapeDtypeStruct((width, columns), F32),
         ],
         scratch_shapes=[pltpu.VMEM((rows, LANES), F32)] * 2
-        + [pltpu.VMEM((rows, width), F32), pltpu.VMEM((width, block), F32)],
+        + [pltpu.VMEM((rows, width), F32), pltpu.VMEM((rows, block), BF16)],
         compiler_params=params(),
         cost_estimate=cost(4 * rows * width * columns, 4 * rows * columns, 0),
     )(expo, raised, v, live, weight, sums, student_t, proto)
@@ -336,24 +332,73 @@
     pl.semaphore_wait(barrier, many)
 
 
-def exchange(axis, n, source, landing, send, recv):
+def copies(axis, n, source, landing, send, recv):
     me = lax.axis_index(axis)
 
     def copy(peer, slot):
         return pltpu.make_async_remote_copy(
             src_ref=source(peer),
-            dst_ref=landing.at[slot],
-            send_sem=send.at[peer],
-            recv_sem=recv.at[slot],
+            dst_ref=landing(slot),
+            send_sem=send(peer),
+            recv_sem=recv(slot),
             device_id={axis: peer},
             device_id_type=MESH,
         )
 
-    for step in range(1, n):
-        copy(lax.rem(me + step, n), me).start()
-    for step in range(1, n):
-        peer = lax.rem(me + step, n)
-        copy(peer, peer).wait()
+    def start():
+        for step in range(1, n):
+            copy(lax.rem(me + step, n), me).start()
+
+    def wait():
+        for step in range(1, n):
+            peer = lax.rem(me + step, n)
+            copy(peer, peer).wait()
+
+    return start, wait
+
+
+def exchange(axis, n, source, landing, send, recv):
+    start, wait = copies(
+        axis, n, source, lambda slot: landing.at[slot], lambda peer: send.at[peer], lambda slot: recv.at[slot]
+    )
+    start()
+    wait()
+
+
+def gather_kernel(groups, count, *refs):
+    values, outs, (send, recv) = refs[:count], refs[count : 2 * count], refs[2 * count :]
+    n = groups["dp"]
+    me = lax.axis_index("dp")
+    greet({"dp": n, "tensor": 1}, n - 1)
+    waits = []
+    for k in range(count):
+        start, wait = copies(
+            "dp",
+            n,
+            lambda peer, k=k: values[k],
+            lambda slot, k=k: outs[k].at[slot],
+            lambda peer, k=k: send.at[k, peer],
+            lambda slot, k=k: recv.at[k, slot],
+        )
+        start()
+        waits.append(wait)
+    for k in range(count):
+        outs[k][me] = values[k][...]
+    for wait in waits:
+        wait()
+
+
+def gather_rows(values, groups, ident):
+    n = groups["dp"]
+    return pl.pallas_call(
+        functools.partial(gather_kernel, groups, len(values)),
+        name=f"gather_rows_{ident}",
+        in_specs=[pl.BlockSpec(memory_space=pltpu.VMEM)] * len(values),
+        out_specs=[pl.BlockSpec(memory_space=pltpu.VMEM)] * len(values),
+        out_shape=[jax.ShapeDtypeStruct((n,) + value.shape, value.dtype) for value in values],
+        scratch_shapes=[pltpu.SemaphoreType.DMA((len(values), n))] * 2,
+        compiler_params=pltpu.CompilerParams(collective_id=ident, has_side_effects=True),
+    )(*values)
 
 
 def total_kernel(groups, value, out, near, far, send_a, recv_a, send_b, recv_b):
@@ -393,20 +438,62 @@
     )(value)
 
 
-def owner_kernel(groups, value, out, near, far, part, send_a, recv_a, send_b, recv_b):
+def run_jobs(groups, jobs, send_a, recv_a, send_b, recv_b):
     n, m = groups["dp"], groups["tensor"]
+    me = lax.axis_index("dp")
     greet(groups, n + m - 2)
-    me = lax.axis_index("dp")
-    exchange("dp", n, lambda peer: value.at[peer], near, send_a, recv_a)
-    near[me] = value[me]
-    total = near[0].astype(F32)
-    for slot in range(1, n):
-        total = total + near[slot].astype(F32)
-    part[...] = total.astype(BF16)
-    exchange("tensor", m, lambda peer: part, far, send_b, recv_b)
-    far[lax.axis_index("tensor")] = part[...]
+    firsts, seconds = [], []
+    for k, (source, near, part, far) in enumerate(jobs):
+        start, wait = copies(
+            "dp", n, source, near, lambda peer, k=k: send_a.at[k, peer], lambda slot, k=k: recv_a.at[k, slot]
+        )
+        start()
+        firsts.append(wait)
+    for k, (source, near, part, far) in enumerate(jobs):
+        firsts[k]()
+        total = source(me)[...].astype(F32)
+        for step in range(1, n):
+            total = total + near(lax.rem(me + step, n))[...].astype(F32)
+        part[...] = total.astype(BF16)
+        start, wait = copies(
+            "tensor",
+            m,
+            lambda peer, part=part: part,
+            far,
+            lambda peer, k=k: send_b.at[k, peer],
+            lambda slot, k=k: recv_b.at[k, slot],
+        )
+        start()
+        far(lax.axis_index("tensor"))[...] = part[...]
+        seconds.append(wait)
+    for wait in seconds:
+        wait()
+
+
+def job_semaphores(groups, jobs):
+    n, m = groups["dp"], groups["tensor"]
+    return [pltpu.SemaphoreType.DMA((jobs, n))] * 2 + [pltpu.SemaphoreType.DMA((jobs, m))] * 2
+
+
+OWNER_PIECES = 4
+
+
+def owner_kernel(groups, value, out, near, far, part, *semaphores):
+    rows = out.shape[0] // OWNER_PIECES
+    jobs = []
+    for k in range(OWNER_PIECES):
+        piece = pl.ds(k * rows, rows)
+        jobs.append(
+            (
+                lambda peer, piece=piece: value.at[peer, piece, :],
+                lambda slot, piece=piece: near.at[slot, piece, :],
+                part.at[piece, :],
+                lambda slot, piece=piece: far.at[slot, piece, :],
+            )
+        )
+    run_jobs(groups, jobs, *semaphores)
     total = far[0].astype(F32)
-    for slot in range(1, m):
+    for slot in range(1, groups["tensor"]):
         total = total + far[slot].astype(F32)
     out[...] = total
 
@@ -424,13 +511,53 @@
             pltpu.VMEM((n,) + own, BF16),
             pltpu.VMEM((m,) + own, BF16),
             pltpu.VMEM(own, BF16),
-            pltpu.SemaphoreType.DMA((n,)),
-            pltpu.SemaphoreType.DMA((n,)),
-            pltpu.SemaphoreType.DMA((m,)),
-            pltpu.SemaphoreType.DMA((m,)),
-        ],
+        ]
+        + job_semaphores(groups, OWNER_PIECES),
         compiler_params=pltpu.CompilerParams(collective_id=ident, has_side_effects=True),
     )(value)
+
+
+def head_kernel(groups, wide, narrow, wide_out, narrow_out, wide_near, narrow_near, wide_part, narrow_part, *semaphores):
+    mine = lax.axis_index("tensor")
+    jobs = [
+        (
+            lambda peer: narrow.at[peer, mine],
+            lambda slot: narrow_near.at[slot],
+            narrow_part,
+            lambda slot: narrow_out.at[slot],
+        )
+    ]
+    for k in range(wide.shape[2] // LANES):
+        piece = pl.ds(k * LANES, LANES)
+        jobs.append(
+            (
+                lambda peer, piece=piece: wide.at[peer, :, piece],
+                lambda slot, piece=piece: wide_near.at[slot, :, piece],
+                wide_part.at[:, piece],
+                lambda slot, piece=piece: wide_out.at[slot, :, piece],
+            )
+        )
+    run_jobs(groups, jobs, *semaphores)
+
+
+def head_totals(wide, narrow, groups, ident):
+    n, m = groups["dp"], groups["tensor"]
+    wide_own, narrow_own = wide.shape[1:], narrow.shape[2:]
+    return pl.pallas_call(
+        functools.partial(head_kernel, groups),
+        name="head_totals",
+        in_specs=[pl.BlockSpec(memory_space=pltpu.VMEM)] * 2,
+        out_specs=[pl.BlockSpec(memory_space=pltpu.VMEM)] * 2,
+        out_shape=[jax.ShapeDtypeStruct((m,) + wide_own, BF16), jax.ShapeDtypeStruct((m,) + narrow_own, BF16)],
+        scratch_shapes=[
+            pltpu.VMEM((n,) + wide_own, BF16),
+            pltpu.VMEM((n,) + narrow_own, BF16),
+            pltpu.VMEM(wide_own, BF16),
+            pltpu.VMEM(narrow_own, BF16),
+        ]
+        + job_semaphores(groups, 1 + wide.shape[2] // LANES),
+        compiler_params=pltpu.CompilerParams(collective_id=ident, has_side_effects=True),
+    )(wide, narrow)
 
 
 def head_forward(rows, w_in_all, w_out_all):
@@ -452,8 +579,10 @@
         grad_feats, w_out_all, (((1,), (1,)), ((), ())), preferred_element_type=F32
     )
     grad_pre = (grad_hidden * slope).astype(BF16)
+    width = grad_pre.shape[1] // lax.axis_size("tensor")
+    own_pre = lax.dynamic_slice_in_dim(grad_pre, lax.axis_index("tensor") * width, width, axis=1)
     grad_in_part = lax.dot_general(
-        rows, grad_pre, (((0,), (0,)), ((), ())), preferred_element_type=F32
+        rows, own_pre, (((0,), (0,)), ((), ())), preferred_element_type=F32
     )
     grad_rows = lax.dot_general(
         grad_pre, w_in_all, (((1,), (1,)), ((), ())), preferred_element_type=F32
@@ -491,21 +620,24 @@
     weight = (GRAD_SCALE * jnp.sum(member * inverse[None, :], axis=1)).astype(BF16)
     teacher_pick = jnp.dot(pick, teacher_feats, preferred_element_type=F32)
     teacher_rows = unit_rows(teacher_pick)[0].astype(BF16)
-    teacher_every = lax.all_gather(teacher_rows, "dp", axis=0, tiled=True)
-    weight_every = lax.all_gather(weight, "dp", axis=0, tiled=True).astype(F32)
+    teacher_every, weight_every = gather_rows((teacher_rows, weight.astype(F32).reshape(-1, LANES)), groups, 6)
+    teacher_every = teacher_every.reshape(-1, teacher_rows.shape[1])
     weight_every = weight_every.reshape(-1, LANES)
     live_every = (weight_every > 0).astype(F32)
 
     expo, row_sum = prototype_first(teacher_every, proto_teacher, live_every)
     row_sum = everywhere_total(row_sum, groups, 1)
-
-    rows = jnp.dot(pick, tokens, preferred_element_type=F32).astype(BF16)
-    hidden, slope, unit, inv, student_rows = head_forward(rows, w_in_all, w_out_all)
-    student_every = lax.all_gather(student_rows, "dp", axis=0, tiled=True)
 
     for turn in range(ROUNDS - 2):
         row_sum = prototype_middle(expo, live_every, row_sum)
         row_sum = everywhere_total(row_sum, groups, 2 + turn)
+
+    rows = jnp.dot(pick, tokens, preferred_element_type=F32).astype(BF16)
+    rows, row_sum = lax.optimization_barrier((rows, row_sum))
+    hidden, slope, unit, inv, student_rows = head_forward(rows, w_in_all, w_out_all)
+    (student_every,) = gather_rows((student_rows,), groups, 7)
+    student_every = student_every.reshape(-1, student_rows.shape[1])
+
     raised, v, sums = prototype_last(expo, live_every, row_sum, student_every, proto_student)
     sums = everywhere_total(sums, groups, ROUNDS)
     grad_part, grad_proto = prototype_grad(
@@ -528,10 +660,12 @@
     grad_in_part, grad_out_part, grad_rows = head_backward(
         rows, hidden, slope, unit, inv, grad_unit, w_in_all, w_out_all
     )
-    grad_in, grad_out = (
-        lax.psum_scatter(grad_in_part.astype(BF16), "dp", scatter_dimension=0, tiled=True).astype(F32),
-        lax.psum_scatter(grad_out_part.astype(BF16), "dp", scatter_dimension=0, tiled=True).astype(F32),
-    )
+    n, m = groups["dp"], groups["tensor"]
+    wide = grad_in_part.astype(BF16).reshape(n, -1, grad_in_part.shape[1])
+    narrow = grad_out_part.astype(BF16).reshape(n, m, -1, grad_out_part.shape[1])
+    wide, narrow = head_totals(wide, narrow, groups, ROUNDS + 5)
+    grad_in = wide.transpose(1, 0, 2).reshape(wide.shape[1], -1).astype(F32)
+    grad_out = narrow.reshape(-1, narrow.shape[2]).astype(F32)
     d_tokens = lax.dot_general(
         place, grad_rows.astype(BF16), (((0,), (0,)), ((), ())), preferred_element_type=F32
     ).astype(BF16)

time: 391 us -> 307 us (0.79)
  waiting for transfers between devices: 154 us -> 1.38 us
  Pallas kernels: 157 us -> 240 us
  blocking collectives: 9.01 us -> 0 us
  matrix products: 31.5 us -> 25.1 us
    reduce_scatter x2 -> x0, waiting for transfers between devices: 81.9 us -> none  [the longest x1 63.6 us: shards(): lax.psum_scatter(grad_in_part.astype(BF16), 'dp', scatter_dimension=0, ti...]
    pallas_call x0 -> x3, Pallas kernels: none -> 78.4 us  [the longest x2 44.7 us: gather_rows(): pl.pallas_call(functools.partial(gather_kernel, groups, len(values)), nam...]
    all_gather x1, waiting for transfers between devices: 39.7 us -> 0.01 us  [shards(): w_in_all = lax.all_gather(w_in, 'dp', axis=0, tiled=True)]
    all_gather x1, waiting for transfers between devices: 19 us -> 0.01 us  [shards(): w_out_all = lax.all_gather(w_out, 'dp', axis=0, tiled=True)]
    all_gather x2 -> x0, waiting for transfers between devices: 12.2 us -> none  [the longest x1 12.2 us: shards(): teacher_every = lax.all_gather(teacher_rows, 'dp', axis=0, tiled=True)]
    all_gather x1 -> x0, blocking collectives: 9.01 us -> none  [shards(): weight_every = lax.all_gather(weight, 'dp', axis=0, tiled=True).astype(F32)]
    pallas_call x1, Pallas kernels: 25.7 us -> 34.1 us  [prototype_first(): pl.pallas_call(first_kernel, name='first_round', grid=(columns // block,)...]
    pallas_call x1, Pallas kernels: 12.7 us -> 17.9 us  [prototype_middle(): pl.pallas_call(middle_kernel, name='middle_round', grid=(columns // block...]
  transfers between devices with their start and end apart: 6 -> 2, of which waited for: 5 -> 0; matrix products, arithmetic and copies ran while one was open for 10% -> 6% of each run, Pallas kernels for 15% -> 33%
where the time goes in v2:
time: 307 us; the launch traced here: 306 us
  Pallas kernels  240 us (78%)
  matrix products  25.1 us (8%)
  between operations  14.4 us (5%)
  local copies, waits for them, and re-layouts  13.9 us (5%)
  other arithmetic  10.9 us (4%)
    pallas_call x2, Pallas kernels, gather_rows(): pl.pallas_call(functools.partial(gather_kernel, groups, len(values)), nam...  44.7 us
    pallas_call x1, Pallas kernels, prototype_first(): pl.pallas_call(first_kernel, name='first_round', grid=(columns // block,)...  34.1 us
    pallas_call x1, Pallas kernels, head_totals(): pl.pallas_call(functools.partial(head_kernel, groups), name='head_totals'...  33.7 us
    pallas_call x3, Pallas kernels, everywhere_total(): pl.pallas_call(functools.partial(total_kernel, groups), name=f'row_total_...  31.2 us
    pallas_call x1, Pallas kernels, prototype_grad(): pl.pallas_call(grad_kernel, name='score_grad', grid=(columns // block,),...  29 us
    pallas_call x1, Pallas kernels, prototype_last(): pl.pallas_call(last_kernel, name='last_round', grid=(columns // block,),...  25.4 us
    pallas_call x1, Pallas kernels, owner_total(): pl.pallas_call(functools.partial(owner_kernel, groups), name='owner_total...  24.1 us
    pallas_call x1, Pallas kernels, prototype_middle(): pl.pallas_call(middle_kernel, name='middle_round', grid=(columns // block...  17.9 us
  transfers between devices with their start and end apart: 2, of which 0 were waited for; matrix products, arithmetic and copies ran while one was open for 6% of the time, Pallas kernels for 33%

profile of v2, /device:TPU:1, one launch (start us, length us, event | category | flops | bytes accessed | tf_op | source)
XLA Modules:
  0.0 305.9 jit_solution(4557144509156811598)
XLA Ops:
  8.7 1.4 fusion.35
  12.5 2.3 multiply_reduce_fusion.2
  16.7 27.0 %gather_rows_6.1 = (bf16[8,256,256]{2,1,0:T(8,128)(2,1)}, f32[8,2,128]{2,1,0:T(2,128)}) custom-call(bf16[256,256]{1,0:T(8,128)(2,1)} %multiply_convert_fusion.2.refs_0_, f32[2,128]{1,0:T(2,128)} %fusion.34.refs_1_), custom_call_target="tpu_custom_call" | custom-call | tf_op jit(solution)/shard_map/gather_rows_6/pallas_call | solution.py:393
  44.4 1.6 copy-done.13
  47.2 34.1 %first_round.1 = (bf16[2048,4096]{1,0:T(8,128)(2,1)}, f32[16,128]{1,0:T(8,128)S(1)}) custom-call(bf16[2048,256]{1,0:T(8,128)(2,1)S(1)} %bitcast.67, bf16[256,4096]{1,0:T(8,128)(2,1)S(1)} %copy-done.13, f32[16,128]{1,0:T(8,128)S(1)} %compare_convert_fusion.live), custom_call_target="tpu_custom_call" | custom-call | flops 4294967296 | bytes 16777216 | tf_op jit(solution)/shard_map/first_round/pallas_call | solution.py:238
  81.9 10.4 %row_total_1.1.row_sum = f32[16,128]{1,0:T(8,128)} custom-call(f32[16,128]{1,0:T(8,128)} %copy-done.12), custom_call_target="tpu_custom_call" | custom-call | tf_op jit(solution)/shard_map/row_total_1/pallas_call | solution.py:423
  93.0 17.9 %middle_round.1.value = f32[16,128]{1,0:T(8,128)S(1)} custom-call(bf16[2048,4096]{1,0:T(8,128)(2,1)} %get-tuple-element.20.expo, f32[16,128]{1,0:T(8,128)S(1)} %compare_convert_fusion.live, f32[16,128]{1,0:T(8,128)S(1)} %copy-done.9), custom_call_target="tpu_custom_call" | custom-call | flops 33554432 | bytes 16777216 | tf_op jit(solution)/shard_map/middle_round/pallas_call | solution.py:254
  111.5 10.3 %row_total_2.1.row_sum = f32[16,128]{1,0:T(8,128)} custom-call(f32[16,128]{1,0:T(8,128)} %copy-done.10), custom_call_target="tpu_custom_call" | custom-call | tf_op jit(solution)/shard_map/row_total_2/pallas_call | solution.py:423
  121.8 2.0 convolution_convert_fusion.4
  123.8 6.3 %multiply_convert_fusion = (bf16[256,2048]{1,0:T(8,128)(2,1)S(1)}, f32[256,2048]{1,0:T(8,128)}) fusion(bf16[256,1536]{1,0:T(8,128)(2,1)} %convolution_convert_fusion.4, bf16[1536,2048]{1,0:T(8,128)(2,1)} %all-gather.3.cloned.1.call-done), kind=kOutput, calls=%fused_computation.14 | convolution fusion | flops 1613234176 | bytes 10223616 | tf_op jit(solution)/shard_map/dot_general | solution.py:564
  130.1 2.1 multiply_reduce_fusion.1
  133.2 17.7 %gather_rows_7.1 = bf16[8,256,256]{2,1,0:T(8,128)(2,1)} custom-call(bf16[256,256]{1,0:T(8,128)(2,1)} %multiply_convert_fusion.3.refs_0_), custom_call_target="tpu_custom_call" | custom-call | tf_op jit(solution)/shard_map/gather_rows_7/pallas_call | solution.py:393
  151.0 2.4 copy.26
  153.3 25.4 %last_round.1 = (bf16[2048,4096]{1,0:T(8,128)(2,1)}, f32[8,4096]{1,0:T(8,128)S(1)}, f32[48,128]{1,0:T(8,128)S(1)}) custom-call(bf16[2048,4096]{1,0:T(8,128)(2,1)} %get-tuple-element.20.expo, f32[16,128]{1,0:T(8,128)S(1)} %compare_convert_fusion.live, f32[16,128]{1,0:T(8,128)S(1)} %copy-done.8, bf16[2048,256]{1,0:T(8,128)(2,1)S(1)} %bitcast.62, ...), custom_call_target="tpu_custom_call" | custom-call | flops 4294967296 | bytes 33554432 | tf_op jit(solution)/shard_map/last_round/pallas_call | solution.py:272
  179.4 10.5 %row_total_3.1.sums = f32[48,128]{1,0:T(8,128)} custom-call(f32[48,128]{1,0:T(8,128)} %copy-done.11), custom_call_target="tpu_custom_call" | custom-call | tf_op jit(solution)/shard_map/row_total_3/pallas_call | solution.py:423
  193.3 29.0 %score_grad.1 = (bf16[2048,256]{1,0:T(8,128)(2,1)S(1)}, f32[256,4096]{1,0:T(8,128)}) custom-call(bf16[2048,4096]{1,0:T(8,128)(2,1)} %get-tuple-element.20.expo, bf16[2048,4096]{1,0:T(8,128)(2,1)} %get-tuple-element.24.raised, f32[8,4096]{1,0:T(8,128)S(1)} %get-tuple-element.25.v_in, f32[16,128]{1,0:T(8,128)S(1)} %compare_convert_fusion.live, ...), custom_call_target="tpu_custom_call" | custom-call | flops 8589934592 | bytes 33554432 | tf_op jit(solution)/shard_map/score_grad/pallas_call | solution.py:299
  223.3 24.1 %owner_total.1 = f32[256,256]{1,0:T(8,128)} custom-call(bf16[8,256,256]{2,1,0:T(8,128)(2,1)} %bitcast.64), custom_call_target="tpu_custom_call" | custom-call | tf_op jit(solution)/shard_map/owner_total/pallas_call | solution.py:504
  249.8 1.5 convolution_convert_fusion.2
  251.3 1.3 fusion.1
  252.6 1.8 convolution_convert_fusion.1
  254.4 33.7 %head_totals.1 = (bf16[4,192,512]{2,1,0:T(8,128)(2,1)}, bf16[4,64,256]{2,1,0:T(8,128)(2,1)}) custom-call(bf16[8,192,512]{2,1,0:T(8,128)(2,1)} %bitcast.68, bf16[8,4,64,256]{3,2,1,0:T(8,128)(2,1)} %bitcast.69), custom_call_target="tpu_custom_call" | custom-call | tf_op jit(solution)/shard_map/head_totals/pallas_call | solution.py:546
  288.1 1.3 convert_bitcast_fusion
  289.5 1.3 copy.27
  291.5 7.6 %convolution_convert_fusion = bf16[1024,1536]{1,0:T(8,128)(2,1)} fusion(bf16[256,2048]{1,0:T(8,128)(2,1)} %copy-done.22, bf16[1536,2048]{1,0:T(8,128)(2,1)} %all-gather.3.cloned.1.call-done, s32[1024]{0:T(1024)S(1)} %copy-done.25, pred[1024]{0:T(1024)(128)(4,1)S(1)} %copy-done.27), kind=kOutput, calls=%fused_computation.2 | convolution fusion | flops 2418409472 | bytes 10490880 | tf_op jit(solution)/shard_map/dot_general | solution.py:669
  (89 shorter events, 18.6 us)
Async XLA Ops:
  7.2 114.7 %copy-start = (bf16[1024,1536]{1,0:T(8,128)(2,1)S(1)}, bf16[1024,1536]{1,0:T(8,128)(2,1)}, u32[]{:S(2)}) copy-start(bf16[1024,1536]{1,0:T(8,128)(2,1)} %param.7) | copy-start | bytes 9437188
  7.2 116.6 %all-gather.3.cloned.1.call-start = ((), (), s32[]{:S(2)}) async-start(), calls=%async_computation | async-start | bytes 7077888 | tf_op jit(solution)/shard_map/all_gather | solution.py:609
  7.9 122.2 %all-gather.5.cloned.1.call-start = ((), (), s32[]{:S(2)}) async-start(), calls=%async_computation.1 | async-start | bytes 1179648 | tf_op jit(solution)/shard_map/all_gather | solution.py:610
  11.8 110.0 %copy-start.24 = (s32[1024]{0:T(1024)}, s32[1024]{0:T(1024)S(1)}, u32[]{:S(2)}) copy-start(s32[1024]{0:T(1024)S(1)} %convert_element_type.86) | copy-start | bytes 12292
  12.5 109.3 %copy-start.26 = (pred[1024]{0:T(1024)(128)(4,1)}, pred[1024]{0:T(1024)(128)(4,1)S(1)}, u32[]{:S(2)}) copy-start(pred[1024]{0:T(1024)(128)(4,1)S(1)} %gt.24) | copy-start | bytes 3076
  44.4 1.6 copy-start.13
  46.0 1.2 copy-start.14
  130.1 2.1 copy-start.15
  132.2 21.1 %copy-start.3 = (bf16[256,4096]{1,0:T(8,128)(2,1)S(1)}, bf16[256,4096]{1,0:T(8,128)(2,1)}, u32[]{:S(2)}) copy-start(bf16[256,4096]{1,0:T(8,128)(2,1)} %proto.5) | copy-start | bytes 6291460
  132.2 21.1 %copy-start.8 = (f32[16,128]{1,0:T(8,128)S(1)}, f32[16,128]{1,0:T(8,128)}, u32[]{:S(2)}) copy-start(f32[16,128]{1,0:T(8,128)} %row_total_2.1.row_sum) | copy-start | bytes 24580
  132.4 18.5 %copy-start.23 = (f32[256]{0:T(256)}, f32[256]{0:T(256)S(1)}, u32[]{:S(2)}) copy-start(f32[256]{0:T(256)S(1)} %add_rsqrt_fusion) | copy-start | bytes 3076
  150.9 2.4 copy-start.2
  153.3 38.0 %copy-start.7 = (f32[8,2,128]{2,1,0:T(2,128)S(1)}, f32[8,2,128]{2,1,0:T(2,128)}, u32[]{:S(2)}) copy-start(f32[8,2,128]{2,1,0:T(2,128)} %get-tuple-element.19) | copy-start | bytes 24580
  191.3 1.2 copy-start.4
  193.3 54.1 %copy-start.18 = (f32[256,256]{1,0:T(8,128)S(1)}, f32[256,256]{1,0:T(8,128)}, u32[]{:S(2)}) copy-start(f32[256,256]{1,0:T(8,128)} %copy-done.17) | copy-start | bytes 786436
  223.3 26.5 %copy-start.16 = (bf16[256,2048]{1,0:T(8,128)(2,1)S(1)}, bf16[256,2048]{1,0:T(8,128)(2,1)}, u32[]{:S(2)}) copy-start(bf16[256,2048]{1,0:T(8,128)(2,1)} %copy-done.15) | copy-start | bytes 3145732
  223.3 28.0 %copy-start.19 = (bf16[2048,256]{1,0:T(8,128)(2,1)S(1)}, bf16[2048,256]{1,0:T(8,128)(2,1)}, u32[]{:S(2)}) copy-start(bf16[2048,256]{1,0:T(8,128)(2,1)} %all-gather.5.cloned.1.call-done) | copy-start | bytes 3145732
  247.4 3.9 %copy-start.28 = (f32[256,2048]{1,0:T(8,128)S(1)}, f32[256,2048]{1,0:T(8,128)}, u32[]{:S(2)}) copy-start(f32[256,2048]{1,0:T(8,128)} %get-tuple-element.40) | copy-start | bytes 6291460
  251.3 1.3 copy-start.20
  252.6 1.8 copy-start.22
  289.4 1.3 copy-start.21
  289.4 2.1 copy-start.25
  289.4 2.1 copy-start.27
  291.5 7.6 %copy-start.1 = (bf16[1024,1536]{1,0:T(8,128)(2,1)S(1)}, bf16[1024,1536]{1,0:T(8,128)(2,1)}, u32[]{:S(2)}) copy-start(bf16[1024,1536]{1,0:T(8,128)(2,1)} %param.7) | copy-start | bytes 9437188
  (7 other events, 5.0 us)
Sparse Core Ops, SparseCore 0:
  9.9 59.1 all-gather.2
  71.0 23.4 all-gather.4

commit v3 on v2

--- a/solution.py
+++ b/solution.py
@@ -16,7 +16,10 @@
 GRAD_SCALE = 65536.0
 LOG2E = 1.4426950408889634
 LANES = 128
-BLOCK = 512
+BLOCK = 1 << 21
+TILE = 256
+UNROLL = 4
+ROW_PRODUCT = False
 MESH = pl.DeviceIdType.MESH
 F32 = jnp.float32
 BF16 = jnp.bfloat16
@@ -63,7 +66,11 @@
 
 
 def chunk(step):
-    return pl.ds(pl.multiple_of(step * CAP, CAP), CAP)
+    return pl.ds(pl.multiple_of(step * TILE, TILE), TILE)
+
+
+def each_tile(rows, body):
+    lax.fori_loop(0, rows // TILE, body, 0, unroll=UNROLL)
 
 
 def two_terms(row):
@@ -90,12 +97,15 @@
 
     def sum_rows(step, carry):
         part = chunk(step)
-        acc[part, :] += lax.dot_general(
-            expo[part, :], terms, (((1,), (1,)), ((), ())), preferred_element_type=F32
-        )
+        if ROW_PRODUCT:
+            acc[part, :] += lax.dot_general(
+                expo[part, :], terms, (((1,), (1,)), ((), ())), preferred_element_type=F32
+            )
+        else:
+            acc[part, :] += fold_lanes(expo[part, :].astype(F32) * scale)
         return carry
 
-    lax.fori_loop(0, expo.shape[0] // CAP, sum_rows, 0)
+    each_tile(expo.shape[0], sum_rows)
 
 
 def first_kernel(teach, proto, live, expo, sums, u_terms, acc):
@@ -115,7 +125,7 @@
         expo[part, :] = jnp.exp2(cos * (LOG2E / TEACHER_TEMP)).astype(BF16)
         return carry
 
-    lax.fori_loop(0, rows // CAP, raise_rows, 0)
+    each_tile(rows, raise_rows)
     add_row_sums(expo, column_scale(expo, u_terms), acc)
 
     @pl.when(here == pl.num_programs(0) - 1)
@@ -164,7 +174,7 @@
         acc_c[part, :] += fold_lanes(balanced * dots)
         return carry
 
-    lax.fori_loop(0, rows // CAP, sum_rows, 0)
+    each_tile(rows, sum_rows)
 
     @pl.when(here == pl.num_programs(0) - 1)
     def _():
@@ -204,7 +214,7 @@
         )
         return carry
 
-    lax.fori_loop(0, rows // CAP, one_group, 0)
+    each_tile(rows, one_group)
     grad = jnp.dot(student_t[...], score[...], preferred_element_type=F32)
     grad_out[...] = (grad - unit * jnp.sum(unit * grad, axis=0, keepdims=True)) / norms
 
@@ -234,7 +244,7 @@
 def prototype_first(teach, proto, live):
     rows, width = teach.shape
     columns = proto.shape[1]
-    block = min(BLOCK, columns)
+    block = min(BLOCK // rows, columns)
     return pl.pallas_call(
         first_kernel,
         name="first_round",
@@ -242,7 +252,7 @@
         in_specs=[whole(teach.shape), tall(width, block), whole(live.shape)],
         out_specs=[tall(rows, block), whole(live.shape)],
         out_shape=[jax.ShapeDtypeStruct((rows, columns), BF16), jax.ShapeDtypeStruct(live.shape, F32)],
-        scratch_shapes=[pltpu.VMEM((16, rows), BF16), pltpu.VMEM((rows, 16), F32)],
+        scratch_shapes=[pltpu.VMEM((16, rows), BF16), pltpu.VMEM((rows, 16 if ROW_PRODUCT else LANES), F32)],
         compiler_params=params(),
         cost_estimate=cost(2 * rows * width * columns, 2 * rows * columns, rows * columns),
     )(teach, proto, live)
@@ -250,7 +260,7 @@
 
 def prototype_middle(expo, live, row_sum):
     rows, columns = expo.shape
-    block = min(BLOCK, columns)
+    block = min(BLOCK // rows, columns)
     return pl.pallas_call(
         middle_kernel,
         name="middle_round",
@@ -258,7 +268,7 @@
         in_specs=[tall(rows, block), whole(live.shape), whole(live.shape)],
         out_specs=whole(live.shape),
         out_shape=jax.ShapeDtypeStruct(live.shape, F32),
-        scratch_shapes=[pltpu.VMEM((16, rows), BF16), pltpu.VMEM((rows, 16), F32)],
+        scratch_shapes=[pltpu.VMEM((16, rows), BF16), pltpu.VMEM((rows, 16 if ROW_PRODUCT else LANES), F32)],
         compiler_params=params(),
         cost_estimate=cost(4 * rows * columns, 2 * rows * columns, 0),
     )(expo, live, row_sum)
@@ -267,7 +277,7 @@
 def prototype_last(expo, live, row_sum, student, proto):
     rows, columns = expo.shape
     width = student.shape[1]
-    block = min(BLOCK, columns)
+    block = min(BLOCK // rows, columns)
     dense = live.shape[0]
     return pl.pallas_call(
         last_kernel,
@@ -295,7 +305,7 @@
 def prototype_grad(expo, raised, v, live, weight, sums, student_t, proto):
     rows, columns = expo.shape
     width = proto.shape[0]
-    block = min(BLOCK, columns)
+    block = min(BLOCK // rows, columns)
     return pl.pallas_call(
         grad_kernel,
         name="score_grad",
@@ -606,8 +616,6 @@
 
 
 def shards(groups, tokens, teacher_feats, masks, w_in, w_out, proto_student, proto_teacher):
-    w_in_all = lax.all_gather(w_in, "dp", axis=0, tiled=True)
-    w_out_all = lax.all_gather(w_out, "dp", axis=0, tiled=True)
     pick, place = selection(masks)
     counts = jnp.sum(masks, axis=1)
     ends = jnp.sum(
@@ -621,6 +629,9 @@
     teacher_pick = jnp.dot(pick, teacher_feats, preferred_element_type=F32)
     teacher_rows = unit_rows(teacher_pick)[0].astype(BF16)
     teacher_every, weight_every = gather_rows((teacher_rows, weight.astype(F32).reshape(-1, LANES)), groups, 6)
+    teacher_every, w_in, w_out = lax.optimization_barrier((teacher_every, w_in, w_out))
+    w_in_all = lax.all_gather(w_in, "dp", axis=0, tiled=True)
+    w_out_all = lax.all_gather(w_out, "dp", axis=0, tiled=True)
     teacher_every = teacher_every.reshape(-1, teacher_rows.shape[1])
     weight_every = weight_every.reshape(-1, LANES)
     live_every = (weight_every > 0).astype(F32)

time: 307 us -> 270 us (0.88)
  Pallas kernels: 240 us -> 193 us
  waiting for transfers between devices: 1.38 us -> 11.9 us
    pallas_call x1, Pallas kernels: 34.1 us -> 15.1 us  [prototype_first(): pl.pallas_call(first_kernel, name='first_round', grid=(columns // block,)...]
    all_gather x1, waiting for transfers between devices: 0.01 us -> 11.2 us  [shards(): w_out_all = lax.all_gather(w_out, 'dp', axis=0, tiled=True)]
    pallas_call x2, Pallas kernels: 44.7 us -> 35.4 us  [gather_rows(): pl.pallas_call(functools.partial(gather_kernel, groups, len(values)), nam...]
    pallas_call x1, Pallas kernels: 17.9 us -> 9.59 us  [prototype_middle(): pl.pallas_call(middle_kernel, name='middle_round', grid=(columns // block...]
    pallas_call x1, Pallas kernels: 25.4 us -> 19.2 us  [prototype_last(): pl.pallas_call(last_kernel, name='last_round', grid=(columns // block,),...]
    pallas_call x1, Pallas kernels: 29 us -> 23.3 us  [prototype_grad(): pl.pallas_call(grad_kernel, name='score_grad', grid=(columns // block,),...]
  transfers between devices with their start and end apart: 2 -> 2, of which waited for: 0 -> 1; matrix products, arithmetic and copies ran while one was open for 6% -> 3% of each run, Pallas kernels for 33% -> 17%
where the time goes in v3:
time: 270 us; the launch traced here: 269 us
  Pallas kernels  193 us (71%)
  matrix products  24.6 us (9%)
  between operations  14.4 us (5%)
  local copies, waits for them, and re-layouts  13.9 us (5%)
  waiting for transfers between devices  11.9 us (4%)
  other arithmetic  11 us (4%)
    pallas_call x2, Pallas kernels, gather_rows(): pl.pallas_call(functools.partial(gather_kernel, groups, len(values)), nam...  35.4 us
    pallas_call x1, Pallas kernels, head_totals(): pl.pallas_call(functools.partial(head_kernel, groups), name='head_totals'...  33.2 us
    pallas_call x3, Pallas kernels, everywhere_total(): pl.pallas_call(functools.partial(total_kernel, groups), name=f'row_total_...  33 us
    pallas_call x1, Pallas kernels, owner_total(): pl.pallas_call(functools.partial(owner_kernel, groups), name='owner_total...  24.2 us
    pallas_call x1, Pallas kernels, prototype_grad(): pl.pallas_call(grad_kernel, name='score_grad', grid=(columns // block,),...  23.3 us
    pallas_call x1, Pallas kernels, prototype_last(): pl.pallas_call(last_kernel, name='last_round', grid=(columns // block,),...  19.2 us
    pallas_call x1, Pallas kernels, prototype_first(): pl.pallas_call(first_kernel, name='first_round', grid=(columns // block,)...  15.1 us
    all_gather x1, waiting for transfers between devices, shards(): w_out_all = lax.all_gather(w_out, 'dp', axis=0, tiled=True)  11.2 us
  transfers between devices with their start and end apart: 2, of which 1 were waited for; matrix products, arithmetic and copies ran while one was open for 3% of the time, Pallas kernels for 17%

profile of v3, /device:TPU:1, one launch (start us, length us, event | category | flops | bytes accessed | tf_op | source)
XLA Modules:
  0.0 268.9 jit_solution(6219947687237971269)
XLA Ops:
  7.2 1.5 fusion.35
  11.2 2.3 multiply_reduce_fusion.2
  15.4 18.6 %gather_rows_6.1 = (bf16[8,256,256]{2,1,0:T(8,128)(2,1)}, f32[8,2,128]{2,1,0:T(2,128)}) custom-call(bf16[256,256]{1,0:T(8,128)(2,1)} %multiply_convert_fusion.2.refs_0_, f32[2,128]{1,0:T(2,128)} %fusion.34.refs_1_), custom_call_target="tpu_custom_call" | custom-call | tf_op jit(solution)/shard_map/gather_rows_6/pallas_call | solution.py:403
  35.5 1.6 copy-done.13
  38.3 15.1 %first_round.1 = (bf16[2048,4096]{1,0:T(8,128)(2,1)}, f32[16,128]{1,0:T(8,128)S(1)}) custom-call(bf16[2048,256]{1,0:T(8,128)(2,1)S(1)} %bitcast.67, bf16[256,4096]{1,0:T(8,128)(2,1)S(1)} %copy-done.13, f32[16,128]{1,0:T(8,128)S(1)} %compare_convert_fusion.live), custom_call_target="tpu_custom_call" | custom-call | flops 4294967296 | bytes 16777216 | tf_op jit(solution)/shard_map/first_round/pallas_call | solution.py:248
  53.9 10.9 %row_total_1.1.row_sum = f32[16,128]{1,0:T(8,128)} custom-call(f32[16,128]{1,0:T(8,128)} %copy-done.12), custom_call_target="tpu_custom_call" | custom-call | tf_op jit(solution)/shard_map/row_total_1/pallas_call | solution.py:433
  65.5 9.6 %middle_round.1.value = f32[16,128]{1,0:T(8,128)S(1)} custom-call(bf16[2048,4096]{1,0:T(8,128)(2,1)} %get-tuple-element.24.expo, f32[16,128]{1,0:T(8,128)S(1)} %compare_convert_fusion.live, f32[16,128]{1,0:T(8,128)S(1)} %copy-done.9), custom_call_target="tpu_custom_call" | custom-call | flops 33554432 | bytes 16777216 | tf_op jit(solution)/shard_map/middle_round/pallas_call | solution.py:264
  75.7 10.8 %row_total_2.1.row_sum = f32[16,128]{1,0:T(8,128)} custom-call(f32[16,128]{1,0:T(8,128)} %copy-done.10), custom_call_target="tpu_custom_call" | custom-call | tf_op jit(solution)/shard_map/row_total_2/pallas_call | solution.py:433
  86.5 1.9 convolution_convert_fusion.4
  88.5 6.4 %multiply_convert_fusion = (bf16[256,2048]{1,0:T(8,128)(2,1)S(1)}, f32[256,2048]{1,0:T(8,128)}) fusion(bf16[256,1536]{1,0:T(8,128)(2,1)} %convolution_convert_fusion.4, bf16[1536,2048]{1,0:T(8,128)(2,1)} %all-gather.3.cloned.1.call-done), kind=kOutput, calls=%fused_computation.14 | convolution fusion | flops 1613234176 | bytes 10223616 | tf_op jit(solution)/shard_map/dot_general | solution.py:574
  94.9 11.2 %all-gather.5.cloned.1.call-done = bf16[2048,256]{1,0:T(8,128)(2,1)} async-done(((bf16[256,256]{1,0:T(8,128)(2,1)}), bf16[2048,256]{1,0:T(8,128)(2,1)}) %all-gather.5.cloned.1.call-update) | async-done | bytes 1048592 | tf_op jit(solution)/shard_map/all_gather | solution.py:634
  106.1 1.8 multiply_reduce_fusion.1
  108.8 16.8 %gather_rows_7.1 = bf16[8,256,256]{2,1,0:T(8,128)(2,1)} custom-call(bf16[256,256]{1,0:T(8,128)(2,1)} %multiply_convert_fusion.3.refs_0_), custom_call_target="tpu_custom_call" | custom-call | tf_op jit(solution)/shard_map/gather_rows_7/pallas_call | solution.py:403
  125.6 2.4 copy.26
  128.0 19.2 %last_round.1 = (bf16[2048,4096]{1,0:T(8,128)(2,1)}, f32[8,4096]{1,0:T(8,128)S(1)}, f32[48,128]{1,0:T(8,128)S(1)}) custom-call(bf16[2048,4096]{1,0:T(8,128)(2,1)} %get-tuple-element.24.expo, f32[16,128]{1,0:T(8,128)S(1)} %compare_convert_fusion.live, f32[16,128]{1,0:T(8,128)S(1)} %copy-done.8, bf16[2048,256]{1,0:T(8,128)(2,1)S(1)} %bitcast.62, ...), custom_call_target="tpu_custom_call" | custom-call | flops 4294967296 | bytes 33554432 | tf_op jit(solution)/shard_map/last_round/pallas_call | solution.py:282
  147.8 11.3 %row_total_3.1.sums = f32[48,128]{1,0:T(8,128)} custom-call(f32[48,128]{1,0:T(8,128)} %copy-done.11), custom_call_target="tpu_custom_call" | custom-call | tf_op jit(solution)/shard_map/row_total_3/pallas_call | solution.py:433
  162.6 23.3 %score_grad.1 = (bf16[2048,256]{1,0:T(8,128)(2,1)S(1)}, f32[256,4096]{1,0:T(8,128)}) custom-call(bf16[2048,4096]{1,0:T(8,128)(2,1)} %get-tuple-element.24.expo, bf16[2048,4096]{1,0:T(8,128)(2,1)} %get-tuple-element.30.raised, f32[8,4096]{1,0:T(8,128)S(1)} %get-tuple-element.31.v_in, f32[16,128]{1,0:T(8,128)S(1)} %compare_convert_fusion.live, ...), custom_call_target="tpu_custom_call" | custom-call | flops 8589934592 | bytes 33554432 | tf_op jit(solution)/shard_map/score_grad/pallas_call | solution.py:309
  186.9 24.2 %owner_total.1 = f32[256,256]{1,0:T(8,128)} custom-call(bf16[8,256,256]{2,1,0:T(8,128)(2,1)} %bitcast.64), custom_call_target="tpu_custom_call" | custom-call | tf_op jit(solution)/shard_map/owner_total/pallas_call | solution.py:514
  213.5 1.5 convolution_convert_fusion.2
  216.1 1.8 convolution_convert_fusion.1
  217.9 33.2 %head_totals.1 = (bf16[4,192,512]{2,1,0:T(8,128)(2,1)}, bf16[4,64,256]{2,1,0:T(8,128)(2,1)}) custom-call(bf16[8,192,512]{2,1,0:T(8,128)(2,1)} %bitcast.68, bf16[8,4,64,256]{3,2,1,0:T(8,128)(2,1)} %bitcast.69), custom_call_target="tpu_custom_call" | custom-call | tf_op jit(solution)/shard_map/head_totals/pallas_call | solution.py:556
  251.1 1.3 convert_bitcast_fusion
  252.4 1.3 copy.27
  254.5 7.6 %convolution_convert_fusion = bf16[1024,1536]{1,0:T(8,128)(2,1)} fusion(bf16[256,2048]{1,0:T(8,128)(2,1)} %copy-done.22, bf16[1536,2048]{1,0:T(8,128)(2,1)} %all-gather.3.cloned.1.call-done, s32[1024]{0:T(1024)S(1)} %copy-done.25, pred[1024]{0:T(1024)(128)(4,1)S(1)} %copy-done.27), kind=kOutput, calls=%fused_computation.2 | convolution fusion | flops 2418409472 | bytes 10490880 | tf_op jit(solution)/shard_map/dot_general | solution.py:680
  (89 shorter events, 19.1 us)
Async XLA Ops:
  7.2 79.4 %copy-start = (bf16[1024,1536]{1,0:T(8,128)(2,1)S(1)}, bf16[1024,1536]{1,0:T(8,128)(2,1)}, u32[]{:S(2)}) copy-start(bf16[1024,1536]{1,0:T(8,128)(2,1)} %param.7) | copy-start | bytes 9437188
  7.2 81.3 %all-gather.3.cloned.1.call-start = ((), (), s32[]{:S(2)}) async-start(), calls=%async_computation | async-start | bytes 7077888 | tf_op jit(solution)/shard_map/all_gather | solution.py:633
  10.5 76.0 %copy-start.24 = (s32[1024]{0:T(1024)}, s32[1024]{0:T(1024)S(1)}, u32[]{:S(2)}) copy-start(s32[1024]{0:T(1024)S(1)} %convert_element_type.86) | copy-start | bytes 12292
  11.2 75.3 %copy-start.26 = (pred[1024]{0:T(1024)(128)(4,1)}, pred[1024]{0:T(1024)(128)(4,1)S(1)}, u32[]{:S(2)}) copy-start(pred[1024]{0:T(1024)(128)(4,1)S(1)} %gt.24) | copy-start | bytes 3076
  34.0 72.1 %all-gather.5.cloned.1.call-start = ((), (), s32[]{:S(2)}) async-start(), calls=%async_computation.1 | async-start | bytes 1179648 | tf_op jit(solution)/shard_map/all_gather | solution.py:634
  35.5 1.6 copy-start.13
  37.1 1.2 copy-start.14
  94.9 12.9 %copy-start.15 = (bf16[256,2048]{1,0:T(8,128)(2,1)}, bf16[256,2048]{1,0:T(8,128)(2,1)S(1)}, u32[]{:S(2)}) copy-start(bf16[256,2048]{1,0:T(8,128)(2,1)S(1)} %get-tuple-element.45) | copy-start | bytes 3145732
  107.9 20.1 %copy-start.3 = (bf16[256,4096]{1,0:T(8,128)(2,1)S(1)}, bf16[256,4096]{1,0:T(8,128)(2,1)}, u32[]{:S(2)}) copy-start(bf16[256,4096]{1,0:T(8,128)(2,1)} %proto.5) | copy-start | bytes 6291460
  107.9 20.1 %copy-start.8 = (f32[16,128]{1,0:T(8,128)S(1)}, f32[16,128]{1,0:T(8,128)}, u32[]{:S(2)}) copy-start(f32[16,128]{1,0:T(8,128)} %row_total_2.1.row_sum) | copy-start | bytes 24580
  108.0 17.6 %copy-start.23 = (f32[256]{0:T(256)}, f32[256]{0:T(256)S(1)}, u32[]{:S(2)}) copy-start(f32[256]{0:T(256)S(1)} %add_rsqrt_fusion) | copy-start | bytes 3076
  125.6 2.4 copy-start.2
  128.0 32.6 %copy-start.7 = (f32[8,2,128]{2,1,0:T(2,128)S(1)}, f32[8,2,128]{2,1,0:T(2,128)}, u32[]{:S(2)}) copy-start(f32[8,2,128]{2,1,0:T(2,128)} %get-tuple-element.23) | copy-start | bytes 24580
  160.6 1.2 copy-start.4
  162.6 48.5 %copy-start.18 = (f32[256,256]{1,0:T(8,128)S(1)}, f32[256,256]{1,0:T(8,128)}, u32[]{:S(2)}) copy-start(f32[256,256]{1,0:T(8,128)} %copy-done.17) | copy-start | bytes 786436
  186.9 26.6 %copy-start.16 = (bf16[256,2048]{1,0:T(8,128)(2,1)S(1)}, bf16[256,2048]{1,0:T(8,128)(2,1)}, u32[]{:S(2)}) copy-start(bf16[256,2048]{1,0:T(8,128)(2,1)} %copy-done.15) | copy-start | bytes 3145732
  186.9 28.1 %copy-start.19 = (bf16[2048,256]{1,0:T(8,128)(2,1)S(1)}, bf16[2048,256]{1,0:T(8,128)(2,1)}, u32[]{:S(2)}) copy-start(bf16[2048,256]{1,0:T(8,128)(2,1)} %all-gather.5.cloned.1.call-done) | copy-start | bytes 3145732
  211.1 3.9 %copy-start.28 = (f32[256,2048]{1,0:T(8,128)S(1)}, f32[256,2048]{1,0:T(8,128)}, u32[]{:S(2)}) copy-start(f32[256,2048]{1,0:T(8,128)} %get-tuple-element.46) | copy-start | bytes 6291460
  215.0 1.1 copy-start.20
  216.1 1.8 copy-start.22
  252.4 1.3 copy-start.21
  252.4 2.1 copy-start.25
  252.4 2.1 copy-start.27
  254.5 7.6 %copy-start.1 = (bf16[1024,1536]{1,0:T(8,128)(2,1)S(1)}, bf16[1024,1536]{1,0:T(8,128)(2,1)}, u32[]{:S(2)}) copy-start(bf16[1024,1536]{1,0:T(8,128)(2,1)} %param.7) | copy-start | bytes 9437188
  (7 other events, 5.0 us)
Sparse Core Ops, SparseCore 0:
  34.1 46.8 all-gather.2
  82.9 23.1 all-gather.4

commit v4 on v3

--- a/solution.py
+++ b/solution.py
@@ -380,22 +380,33 @@
     n = groups["dp"]
     me = lax.axis_index("dp")
     greet({"dp": n, "tensor": 1}, n - 1)
-    waits = []
+    flip = 1 - 2 * lax.rem(me, 2)
+    partner = me + flip
+    peers = [lax.rem(me + step, n) for step in range(2, n, 2)]
+
+    def copy(k, source, slot, sender, peer):
+        return pltpu.make_async_remote_copy(
+            src_ref=source,
+            dst_ref=outs[k].at[slot],
+            send_sem=send.at[k, sender],
+            recv_sem=recv.at[k, slot],
+            device_id={"dp": peer},
+            device_id_type=MESH,
+        )
+
     for k in range(count):
-        start, wait = copies(
-            "dp",
-            n,
-            lambda peer, k=k: values[k],
-            lambda slot, k=k: outs[k].at[slot],
-            lambda peer, k=k: send.at[k, peer],
-            lambda slot, k=k: recv.at[k, slot],
-        )
-        start()
-        waits.append(wait)
+        for peer in peers + [partner]:
+            copy(k, values[k], me, peer, peer).start()
+        outs[k][me] = values[k][...]
+    for peer in peers:
+        for k in range(count):
+            copy(k, values[k], peer, peer, peer).wait_recv()
+            copy(k, outs[k].at[peer], peer, peer + flip, partner).start()
     for k in range(count):
-        outs[k][me] = values[k][...]
-    for wait in waits:
-        wait()
+        copy(k, values[k], partner, partner, partner).wait()
+        for peer in peers:
+            copy(k, values[k], me, peer, peer).wait_send()
+            copy(k, outs[k].at[peer], peer + flip, peer + flip, partner).wait()
 
 
 def gather_rows(values, groups, ident):

time: 270 us -> 263 us (0.974)
  Pallas kernels: 193 us -> 186 us
    pallas_call x2, Pallas kernels: 35.4 us -> 27.6 us  [gather_rows(): pl.pallas_call(functools.partial(gather_kernel, groups, len(values)), nam...]
  transfers between devices with their start and end apart: 2 -> 2, of which waited for: 1 -> 1; matrix products, arithmetic and copies ran while one was open for 3% -> 3% of each run, Pallas kernels for 17% -> 18%
where the time goes in v4:
time: 263 us; the launch traced here: 262 us
  Pallas kernels  186 us (71%)
  matrix products  24.6 us (9%)
  between operations  14.4 us (5%)
  local copies, waits for them, and re-layouts  13.9 us (5%)
  waiting for transfers between devices  12 us (5%)
  other arithmetic  11 us (4%)
    pallas_call x1, Pallas kernels, head_totals(): pl.pallas_call(functools.partial(head_kernel, groups), name='head_totals'...  34 us
    pallas_call x3, Pallas kernels, everywhere_total(): pl.pallas_call(functools.partial(total_kernel, groups), name=f'row_total_...  32.7 us
    pallas_call x2, Pallas kernels, gather_rows(): pl.pallas_call(functools.partial(gather_kernel, groups, len(values)), nam...  27.6 us
    pallas_call x1, Pallas kernels, owner_total(): pl.pallas_call(functools.partial(owner_kernel, groups), name='owner_total...  24.2 us
    pallas_call x1, Pallas kernels, prototype_grad(): pl.pallas_call(grad_kernel, name='score_grad', grid=(columns // block,),...  23.3 us
    pallas_call x1, Pallas kernels, prototype_last(): pl.pallas_call(last_kernel, name='last_round', grid=(columns // block,),...  19.2 us
    pallas_call x1, Pallas kernels, prototype_first(): pl.pallas_call(first_kernel, name='first_round', grid=(columns // block,)...  15.1 us
    all_gather x1, waiting for transfers between devices, shards(): w_out_all = lax.all_gather(w_out, 'dp', axis=0, tiled=True)  11.3 us
  transfers between devices with their start and end apart: 2, of which 1 were waited for; matrix products, arithmetic and copies ran while one was open for 3% of the time, Pallas kernels for 18%

profile of v4, /device:TPU:1, one launch (start us, length us, event | category | flops | bytes accessed | tf_op | source)
XLA Modules:
  0.0 261.8 jit_solution(10462065331564881298)
XLA Ops:
  7.2 1.5 fusion.35
  11.2 2.3 multiply_reduce_fusion.2
  15.4 14.6 %gather_rows_6.1 = (bf16[8,256,256]{2,1,0:T(8,128)(2,1)}, f32[8,2,128]{2,1,0:T(2,128)}) custom-call(bf16[256,256]{1,0:T(8,128)(2,1)} %multiply_convert_fusion.2.refs_0_, f32[2,128]{1,0:T(2,128)} %fusion.34.refs_1_), custom_call_target="tpu_custom_call" | custom-call | tf_op jit(solution)/shard_map/gather_rows_6/pallas_call | solution.py:414
  31.4 1.6 copy-done.13
  34.2 15.1 %first_round.1 = (bf16[2048,4096]{1,0:T(8,128)(2,1)}, f32[16,128]{1,0:T(8,128)S(1)}) custom-call(bf16[2048,256]{1,0:T(8,128)(2,1)S(1)} %bitcast.67, bf16[256,4096]{1,0:T(8,128)(2,1)S(1)} %copy-done.13, f32[16,128]{1,0:T(8,128)S(1)} %compare_convert_fusion.live), custom_call_target="tpu_custom_call" | custom-call | flops 4294967296 | bytes 16777216 | tf_op jit(solution)/shard_map/first_round/pallas_call | solution.py:248
  49.9 10.6 %row_total_1.1.row_sum = f32[16,128]{1,0:T(8,128)} custom-call(f32[16,128]{1,0:T(8,128)} %copy-done.12), custom_call_target="tpu_custom_call" | custom-call | tf_op jit(solution)/shard_map/row_total_1/pallas_call | solution.py:444
  61.2 9.6 %middle_round.1.value = f32[16,128]{1,0:T(8,128)S(1)} custom-call(bf16[2048,4096]{1,0:T(8,128)(2,1)} %get-tuple-element.24.expo, f32[16,128]{1,0:T(8,128)S(1)} %compare_convert_fusion.live, f32[16,128]{1,0:T(8,128)S(1)} %copy-done.9), custom_call_target="tpu_custom_call" | custom-call | flops 33554432 | bytes 16777216 | tf_op jit(solution)/shard_map/middle_round/pallas_call | solution.py:264
  71.4 10.7 %row_total_2.1.row_sum = f32[16,128]{1,0:T(8,128)} custom-call(f32[16,128]{1,0:T(8,128)} %copy-done.10), custom_call_target="tpu_custom_call" | custom-call | tf_op jit(solution)/shard_map/row_total_2/pallas_call | solution.py:444
  82.2 2.0 convolution_convert_fusion.4
  84.1 6.4 %multiply_convert_fusion = (bf16[256,2048]{1,0:T(8,128)(2,1)S(1)}, f32[256,2048]{1,0:T(8,128)}) fusion(bf16[256,1536]{1,0:T(8,128)(2,1)} %convolution_convert_fusion.4, bf16[1536,2048]{1,0:T(8,128)(2,1)} %all-gather.3.cloned.1.call-done), kind=kOutput, calls=%fused_computation.14 | convolution fusion | flops 1613234176 | bytes 10223616 | tf_op jit(solution)/shard_map/dot_general | solution.py:585
  90.6 11.3 %all-gather.5.cloned.1.call-done = bf16[2048,256]{1,0:T(8,128)(2,1)} async-done(((bf16[256,256]{1,0:T(8,128)(2,1)}), bf16[2048,256]{1,0:T(8,128)(2,1)}) %all-gather.5.cloned.1.call-update) | async-done | bytes 1048592 | tf_op jit(solution)/shard_map/all_gather | solution.py:645
  101.9 1.8 multiply_reduce_fusion.1
  104.6 13.1 %gather_rows_7.1 = bf16[8,256,256]{2,1,0:T(8,128)(2,1)} custom-call(bf16[256,256]{1,0:T(8,128)(2,1)} %multiply_convert_fusion.3.refs_0_), custom_call_target="tpu_custom_call" | custom-call | tf_op jit(solution)/shard_map/gather_rows_7/pallas_call | solution.py:414
  117.7 2.4 copy.26
  120.1 19.2 %last_round.1 = (bf16[2048,4096]{1,0:T(8,128)(2,1)}, f32[8,4096]{1,0:T(8,128)S(1)}, f32[48,128]{1,0:T(8,128)S(1)}) custom-call(bf16[2048,4096]{1,0:T(8,128)(2,1)} %get-tuple-element.24.expo, f32[16,128]{1,0:T(8,128)S(1)} %compare_convert_fusion.live, f32[16,128]{1,0:T(8,128)S(1)} %copy-done.8, bf16[2048,256]{1,0:T(8,128)(2,1)S(1)} %bitcast.62, ...), custom_call_target="tpu_custom_call" | custom-call | flops 4294967296 | bytes 33554432 | tf_op jit(solution)/shard_map/last_round/pallas_call | solution.py:282
  139.9 11.4 %row_total_3.1.sums = f32[48,128]{1,0:T(8,128)} custom-call(f32[48,128]{1,0:T(8,128)} %copy-done.11), custom_call_target="tpu_custom_call" | custom-call | tf_op jit(solution)/shard_map/row_total_3/pallas_call | solution.py:444
  154.7 23.3 %score_grad.1 = (bf16[2048,256]{1,0:T(8,128)(2,1)S(1)}, f32[256,4096]{1,0:T(8,128)}) custom-call(bf16[2048,4096]{1,0:T(8,128)(2,1)} %get-tuple-element.24.expo, bf16[2048,4096]{1,0:T(8,128)(2,1)} %get-tuple-element.30.raised, f32[8,4096]{1,0:T(8,128)S(1)} %get-tuple-element.31.v_in, f32[16,128]{1,0:T(8,128)S(1)} %compare_convert_fusion.live, ...), custom_call_target="tpu_custom_call" | custom-call | flops 8589934592 | bytes 33554432 | tf_op jit(solution)/shard_map/score_grad/pallas_call | solution.py:309
  179.0 24.2 %owner_total.1 = f32[256,256]{1,0:T(8,128)} custom-call(bf16[8,256,256]{2,1,0:T(8,128)(2,1)} %bitcast.64), custom_call_target="tpu_custom_call" | custom-call | tf_op jit(solution)/shard_map/owner_total/pallas_call | solution.py:525
  205.6 1.5 convolution_convert_fusion.2
  208.2 1.8 convolution_convert_fusion.1
  210.0 34.0 %head_totals.1 = (bf16[4,192,512]{2,1,0:T(8,128)(2,1)}, bf16[4,64,256]{2,1,0:T(8,128)(2,1)}) custom-call(bf16[8,192,512]{2,1,0:T(8,128)(2,1)} %bitcast.68, bf16[8,4,64,256]{3,2,1,0:T(8,128)(2,1)} %bitcast.69), custom_call_target="tpu_custom_call" | custom-call | tf_op jit(solution)/shard_map/head_totals/pallas_call | solution.py:567
  244.0 1.3 convert_bitcast_fusion
  245.4 1.3 copy.27
  247.4 7.6 %convolution_convert_fusion = bf16[1024,1536]{1,0:T(8,128)(2,1)} fusion(bf16[256,2048]{1,0:T(8,128)(2,1)} %copy-done.22, bf16[1536,2048]{1,0:T(8,128)(2,1)} %all-gather.3.cloned.1.call-done, s32[1024]{0:T(1024)S(1)} %copy-done.25, pred[1024]{0:T(1024)(128)(4,1)S(1)} %copy-done.27), kind=kOutput, calls=%fused_computation.2 | convolution fusion | flops 2418409472 | bytes 10490880 | tf_op jit(solution)/shard_map/dot_general | solution.py:691
  (89 shorter events, 19.1 us)
Async XLA Ops:
  7.2 75.0 %copy-start = (bf16[1024,1536]{1,0:T(8,128)(2,1)S(1)}, bf16[1024,1536]{1,0:T(8,128)(2,1)}, u32[]{:S(2)}) copy-start(bf16[1024,1536]{1,0:T(8,128)(2,1)} %param.7) | copy-start | bytes 9437188
  7.2 76.9 %all-gather.3.cloned.1.call-start = ((), (), s32[]{:S(2)}) async-start(), calls=%async_computation | async-start | bytes 7077888 | tf_op jit(solution)/shard_map/all_gather | solution.py:644
  10.5 71.6 %copy-start.24 = (s32[1024]{0:T(1024)}, s32[1024]{0:T(1024)S(1)}, u32[]{:S(2)}) copy-start(s32[1024]{0:T(1024)S(1)} %convert_element_type.86) | copy-start | bytes 12292
  11.2 71.0 %copy-start.26 = (pred[1024]{0:T(1024)(128)(4,1)}, pred[1024]{0:T(1024)(128)(4,1)S(1)}, u32[]{:S(2)}) copy-start(pred[1024]{0:T(1024)(128)(4,1)S(1)} %gt.24) | copy-start | bytes 3076
  30.0 71.9 %all-gather.5.cloned.1.call-start = ((), (), s32[]{:S(2)}) async-start(), calls=%async_computation.1 | async-start | bytes 1179648 | tf_op jit(solution)/shard_map/all_gather | solution.py:645
  31.4 1.6 copy-start.13
  33.0 1.2 copy-start.14
  90.5 13.1 %copy-start.15 = (bf16[256,2048]{1,0:T(8,128)(2,1)}, bf16[256,2048]{1,0:T(8,128)(2,1)S(1)}, u32[]{:S(2)}) copy-start(bf16[256,2048]{1,0:T(8,128)(2,1)S(1)} %get-tuple-element.45) | copy-start | bytes 3145732
  103.7 16.4 %copy-start.3 = (bf16[256,4096]{1,0:T(8,128)(2,1)S(1)}, bf16[256,4096]{1,0:T(8,128)(2,1)}, u32[]{:S(2)}) copy-start(bf16[256,4096]{1,0:T(8,128)(2,1)} %proto.5) | copy-start | bytes 6291460
  103.7 16.4 %copy-start.8 = (f32[16,128]{1,0:T(8,128)S(1)}, f32[16,128]{1,0:T(8,128)}, u32[]{:S(2)}) copy-start(f32[16,128]{1,0:T(8,128)} %row_total_2.1.row_sum) | copy-start | bytes 24580
  103.8 13.9 %copy-start.23 = (f32[256]{0:T(256)}, f32[256]{0:T(256)S(1)}, u32[]{:S(2)}) copy-start(f32[256]{0:T(256)S(1)} %add_rsqrt_fusion) | copy-start | bytes 3076
  117.7 2.4 copy-start.2
  120.1 32.7 %copy-start.7 = (f32[8,2,128]{2,1,0:T(2,128)S(1)}, f32[8,2,128]{2,1,0:T(2,128)}, u32[]{:S(2)}) copy-start(f32[8,2,128]{2,1,0:T(2,128)} %get-tuple-element.23) | copy-start | bytes 24580
  152.7 1.2 copy-start.4
  154.7 48.5 %copy-start.18 = (f32[256,256]{1,0:T(8,128)S(1)}, f32[256,256]{1,0:T(8,128)}, u32[]{:S(2)}) copy-start(f32[256,256]{1,0:T(8,128)} %copy-done.17) | copy-start | bytes 786436
  179.0 26.6 %copy-start.16 = (bf16[256,2048]{1,0:T(8,128)(2,1)S(1)}, bf16[256,2048]{1,0:T(8,128)(2,1)}, u32[]{:S(2)}) copy-start(bf16[256,2048]{1,0:T(8,128)(2,1)} %copy-done.15) | copy-start | bytes 3145732
  179.0 28.1 %copy-start.19 = (bf16[2048,256]{1,0:T(8,128)(2,1)S(1)}, bf16[2048,256]{1,0:T(8,128)(2,1)}, u32[]{:S(2)}) copy-start(bf16[2048,256]{1,0:T(8,128)(2,1)} %all-gather.5.cloned.1.call-done) | copy-start | bytes 3145732
  203.2 3.9 %copy-start.28 = (f32[256,2048]{1,0:T(8,128)S(1)}, f32[256,2048]{1,0:T(8,128)}, u32[]{:S(2)}) copy-start(f32[256,2048]{1,0:T(8,128)} %get-tuple-element.46) | copy-start | bytes 6291460
  207.1 1.1 copy-start.20
  208.2 1.8 copy-start.22
  245.3 1.3 copy-start.21
  245.4 2.1 copy-start.25
  245.4 2.1 copy-start.27
  247.4 7.6 %copy-start.1 = (bf16[1024,1536]{1,0:T(8,128)(2,1)S(1)}, bf16[1024,1536]{1,0:T(8,128)(2,1)}, u32[]{:S(2)}) copy-start(bf16[1024,1536]{1,0:T(8,128)(2,1)} %param.7) | copy-start | bytes 9437188
  (7 other events, 5.0 us)
Sparse Core Ops, SparseCore 0:
  30.1 46.6 all-gather.2
  78.7 23.1 all-gather.4
